TPU v7x, 32 devices: a whole 2x2x4 slice. The times are simulated.
32 devices in a mesh: dp: 32 (over z, y, x, core).
Axes of the slice: x: 2, y: 2, z: 4, core: 2. Of those that a mesh axis runs over, the one named last changes fastest.
Arguments:
- images: bfloat16 [256, 196, 512], P('dp'), may hold values from -6 to 6
- cotangent: bfloat16 [256, 196, 512], P('dp'), may hold values from -6 to 6
- image_counts: int32 [32], P('dp'), may hold values from 1 to 8, as said below
- shift_mask: int32 [4, 49, 49], replicated, may hold values from 0 to 1, as said below
- rel_index: int32 [49, 49], replicated, may hold values from 0 to 168
- step_count: int32 [1], replicated, may hold values from 1 to 20
- attend_weight: bfloat16 [512, 1536], P('dp'), may hold values from -0.25 to 0.25
- merge_weight: bfloat16 [512, 512], P('dp'), may hold values from -1 to 1
- expand_weight: bfloat16 [512, 2048], P('dp'), may hold values from -0.25 to 0.25
- project_weight: bfloat16 [2048, 512], P('dp'), may hold values from -0.125 to 0.125
- norm_gains: float32 [2, 512], replicated, may hold values from 0.1 to 1.9
- norm_shifts: float32 [2, 512], replicated, may hold values from -2 to 2
- layer_biases: float32 [4608], replicated, may hold values from -2 to 2
- bias_table: float32 [169, 16], replicated, may hold values from -4 to 4
- attend_momentum: float32 [512, 1536], P('dp'), may hold values from -1.2 to 1.2
- merge_momentum: float32 [512, 512], P('dp'), may hold values from -1.2 to 1.2
- expand_momentum: float32 [512, 2048], P('dp'), may hold values from -1.2 to 1.2
- project_momentum: float32 [2048, 512], P('dp'), may hold values from -1.2 to 1.2
- gains_mean: float32 [2, 512], replicated, may hold values from -0.6 to 0.6
- gains_square: float32 [2, 512], replicated, may hold values from 0.0001 to 0.001
- shifts_mean: float32 [2, 512], replicated, may hold values from -0.6 to 0.6
- shifts_square: float32 [2, 512], replicated, may hold values from 0.0001 to 0.001
- biases_mean: float32 [4608], replicated, may hold values from -0.6 to 0.6
- biases_square: float32 [4608], replicated, may hold values from 0.0001 to 0.001
- table_mean: float32 [169, 16], replicated, may hold values from -0.6 to 0.6
- table_square: float32 [169, 16], replicated, may hold values from 0.0001 to 0.001
Outputs:
- block_out: bfloat16 [256, 196, 512], P('dp')
- input_grad: float32 [256, 196, 512], P('dp')
- attend_grad: float32 [512, 1536], P('dp')
- attend_momentum_next: float32 [512, 1536], P('dp')
- attend_update: float32 [512, 1536], P('dp')
- merge_grad: float32 [512, 512], P('dp')
- merge_momentum_next: float32 [512, 512], P('dp')
- merge_update: float32 [512, 512], P('dp')
- expand_grad: float32 [512, 2048], P('dp')
- expand_momentum_next: float32 [512, 2048], P('dp')
- expand_update: float32 [512, 2048], P('dp')
- project_grad: float32 [2048, 512], P('dp')
- project_momentum_next: float32 [2048, 512], P('dp')
- project_update: float32 [2048, 512], P('dp')
- gains_grad: float32 [2, 512], replicated
- gains_mean_next: float32 [2, 512], replicated
- gains_square_next: float32 [2, 512], replicated
- gains_update: float32 [2, 512], replicated
- shifts_grad: float32 [2, 512], replicated
- shifts_mean_next: float32 [2, 512], replicated
- shifts_square_next: float32 [2, 512], replicated
- shifts_update: float32 [2, 512], replicated
- biases_grad: float32 [4608], replicated
- biases_mean_next: float32 [4608], replicated
- biases_square_next: float32 [4608], replicated
- biases_update: float32 [4608], replicated
- table_grad: float32 [169, 16], replicated
- table_mean_next: float32 [169, 16], replicated
- table_square_next: float32 [169, 16], replicated
- table_update: float32 [169, 16], replicated
Inputs may be any that keep to these rules, and one draw needn't show every extreme that they name: `image_counts`: one device holds 8 live images and another holds 1; live images fill a device's first slots. `shift_mask`: 1 where two patches of a window may attend to each other; symmetric, with ones on the diagonal.
All inputs are finite; a program needn't handle non-finite values.
Results may differ from a plain program's by a relative error of at most 0.0095.
The roundings to bfloat16 on the way count: a program that leaves them out, or rounds other values in their place, can miss the bound.
Values may be sent and summed in bfloat16 or wider, within the bound.
No kernel may reach another device: no remote copies, remote signals or barrier semaphores. Data moves between devices by JAX's collectives and lax.ppermute only.
A program may use at most 256 MiB of HBM per device.

v0:
```python
from functools import partial
import math

import jax
import jax.numpy as jnp
import numpy as np
from jax import lax
from jax.experimental import pallas as pl
from jax.experimental.pallas import tpu as pltpu
from jax.sharding import PartitionSpec as P

HEADS = 16
WIN = 7
SIDE = 14
SHIFT = 3
WIN_TOK = 49
PATCHES = 196
TABLE = 169


newton_first = 3.4445
newton_second = -4.775
newton_third = 2.0315


LANE = 512
CELL = 8
MATRICES = 4


def exchange(payload, devices, mask):
    return lax.ppermute(payload, "dp", [(i, i ^ mask) for i in range(devices)])


def pick(values, index, axis):
    return lax.dynamic_index_in_dim(values, index, axis, keepdims=False)


def split_wide(values):
    high = lax.reduce_precision(values, 8, 7)
    return high.astype(jnp.bfloat16), lax.reduce_precision(values - high, 8, 7).astype(jnp.bfloat16)


def join_wide(high, low):
    return high.astype(jnp.float32) + low.astype(jnp.float32)


def place_rows(rank, sources, outs, spans):
    for number, source in enumerate(sources):
        for plane in range(source.shape[0]):
            owner = jnp.bitwise_xor(rank, number // 4 + 2 * (number % 4) + CELL * plane)
            start = 0
            for out_ref, (blocks, rows) in zip(outs, spans):
                place = pl.ds(pl.multiple_of(owner * rows, rows), rows)
                for block in range(blocks):
                    out_ref[block, place, :] = source[plane, start : start + rows, :]
                    start += rows


def order_rows(sources, spans, rank, devices):
    lanes = sources[0].shape[-1]
    offset = jnp.arange(devices) ^ rank
    both = jnp.stack(sources).reshape(devices, -1, lanes)
    both = jnp.take(both, ((offset & 1) * 4 + ((offset >> 1) & 3)) * (devices // CELL) + (offset >> 3), axis=0)
    out, start = [], 0
    for blocks, rows in spans:
        part = both[:, start : start + blocks * rows].reshape(devices, blocks, rows, lanes)
        out.append(jnp.transpose(part, (1, 0, 2, 3)).reshape(blocks, devices * rows, lanes))
        start += blocks * rows
    return out


def gather_planes(rows, devices):
    return [rows] + [exchange(rows, devices, CELL * step) for step in range(1, devices // CELL)]


def gather_corners(rows, devices):
    return [rows] + [exchange(rows, devices, 2 * step) for step in range(1, 4)]


BODY = ((1, True), (4, False), (4, False))
HEAD = ((3, False),)


def encode(values, spans, rows):
    sent, start = [], 0
    for blocks, wide in spans:
        part = values[..., start : start + blocks * rows, :]
        start += blocks * rows
        high = part.astype(jnp.bfloat16)
        sent.append(high)
        if wide:
            sent.append((part - high.astype(jnp.float32)).astype(jnp.bfloat16))
    return sent[0] if len(sent) == 1 else jnp.concatenate(sent, axis=-2)


def decode(payload, spans, rows):
    out, start = [], 0
    for blocks, wide in spans:
        part = payload[..., start : start + blocks * rows, :].astype(jnp.float32)
        start += blocks * rows
        if wide:
            part = part + payload[..., start : start + blocks * rows, :].astype(jnp.float32)
            start += blocks * rows
        out.append(part)
    return out[0] if len(out) == 1 else jnp.concatenate(out, axis=-2)


def aligned(rows):
    return rows % 16 == 0


def pack_core(parts, spans, rows, mine):
    packed = []
    for (blocks, _), part in zip(spans, parts):
        count = part.shape[0]
        per = blocks * rows // count
        part = part.reshape(count, -1, 2, per, LANE)
        packed.append(jnp.transpose(part, (1, 2, 0, 3, 4)).reshape(part.shape[1], 2, blocks * rows, LANE))
    packed = jnp.concatenate(packed, axis=2)
    return pick(packed, mine, 1), encode(pick(packed, 1 - mine, 1), spans, rows)


def store_core(sources, keep_ref, sent_ref, spans, rows, mine):
    for pair in range(keep_ref.shape[0]):
        start, sent = 0, 0
        for (blocks, wide), (source, count) in zip(spans, sources):
            per = blocks * rows // count
            near = pl.ds(pl.multiple_of(pair * 2 * per + mine * per, per), per)
            away = pl.ds(pl.multiple_of(pair * 2 * per + (1 - mine) * per, per), per)
            for block in range(count):
                lead = (block,) if len(source.shape) == 3 else ()
                keep_ref[pair, start : start + per, :] = source[lead + (near, slice(None))]
                values = source[lead + (away, slice(None))]
                high = values.astype(jnp.bfloat16)
                sent_ref[pair, sent : sent + per, :] = high
                if wide:
                    low = (values - high.astype(jnp.float32)).astype(jnp.bfloat16)
                    sent_ref[pair, sent + blocks * rows : sent + blocks * rows + per, :] = low
                start += per
                sent += per
            if wide:
                sent += blocks * rows


def fold_kernel(own_ref, keep_ref, *refs, gots, spans, rows):
    own = own_ref[0]
    total_ref, *sent_refs = refs[gots:]
    for step in range(keep_ref.shape[1]):
        index = jnp.bitwise_xor(own, step)
        total = keep_ref[0, index]
        for got in refs[:gots]:
            total = total + decode(got[0, index], spans, rows)
        if step:
            sent_refs[step - 1][0] = encode(total, spans, rows)
        else:
            total_ref[0] = total


def fold(keep, got, own, spans, rows):
    groups, members, length, lanes = keep.shape
    if not aligned(rows):
        total = keep
        for payload in got:
            total = total + decode(payload, spans, rows)
        return pick(total, own, 1), [encode(pick(total, own ^ step, 1), spans, rows) for step in range(1, members)]
    sent = got[0].shape[2]

    def block(*shape):
        return pl.BlockSpec((1,) + shape, lambda i: (i,) + (0,) * len(shape))

    total, *sends = pl.pallas_call(
        partial(fold_kernel, gots=len(got), spans=spans, rows=rows),
        grid=(groups,),
        in_specs=[pl.BlockSpec(memory_space=pltpu.SMEM), block(members, length, lanes)]
        + [block(members, sent, lanes)] * len(got),
        out_specs=[block(length, lanes)] + [block(sent, lanes)] * (members - 1),
        out_shape=[jax.ShapeDtypeStruct((groups, length, lanes), jnp.float32)]
        + [jax.ShapeDtypeStruct((groups, sent, lanes), jnp.bfloat16)] * (members - 1),
        compiler_params=pltpu.CompilerParams(vmem_limit_bytes=8 << 20),
        cost_estimate=pl.CostEstimate(flops=2 * 10**9, bytes_accessed=8 * keep.size, transcendentals=0),
        name="fold",
    )(own.reshape(1), keep, *got)
    return total, sends


def send_all(payloads, mask, devices):
    return [exchange(payload, devices, mask * (step + 1)) for step, payload in enumerate(payloads)]


def finish_math(head, head_got, body, body_got, momenta, rows, grad_scale):
    for payload in head_got:
        head = head + decode(payload, HEAD, rows)
    for payload in body_got:
        body = body + decode(payload, BODY, rows)
    spans = (head, body[:rows], body[rows : 5 * rows], body[5 * rows :])
    grads, following, packed = [], [], []
    for order, (span, moment) in enumerate(zip(spans, momenta)):
        blocks = moment.shape[1] // LANE
        per = moment.shape[0]
        grad = jnp.concatenate([span[block * per : (block + 1) * per] for block in range(blocks)], axis=1) * grad_scale
        after = 0.95 * moment + grad
        grads.append(grad)
        following.append(after)
        pieces = [after[:, block * LANE : (block + 1) * LANE] for block in range(blocks)]
        if order == 1:
            high = after.astype(jnp.bfloat16)
            pieces = [high, after - high.astype(jnp.float32)]
        pieces = [piece.astype(jnp.bfloat16) for piece in pieces]
        if per * len(pieces) < 4 * rows:
            pieces.append(jnp.zeros((4 * rows - per * len(pieces), LANE), jnp.bfloat16))
        packed.append(jnp.concatenate(pieces, axis=0))
    return grads, following, packed


def finish_kernel(*refs, count, rows, grad_scale):
    head, body = refs[0][0], refs[1][0]
    head_got = [ref[0] for ref in refs[2 : 2 + count]]
    body_got = [ref[0] for ref in refs[2 + count : 2 + 2 * count]]
    momenta = [ref[...] for ref in refs[2 + 2 * count : 6 + 2 * count]]
    outs = refs[6 + 2 * count :]
    grads, following, packed = finish_math(head, head_got, body, body_got, momenta, rows, grad_scale)
    for index in range(4):
        outs[index][...] = grads[index]
        outs[4 + index][...] = following[index]
        outs[8][index] = packed[index]


def finish(head, head_got, body, body_got, momenta, rows, grad_scale):
    if not aligned(rows):
        grads, following, packed = finish_math(
            head[0], [got[0] for got in head_got], body[0], [got[0] for got in body_got], momenta, rows, grad_scale
        )
        return grads, following, jnp.stack(packed)
    shapes = [jax.ShapeDtypeStruct(moment.shape, jnp.float32) for moment in momenta]
    outs = pl.pallas_call(
        partial(finish_kernel, count=len(head_got), rows=rows, grad_scale=grad_scale),
        out_shape=shapes + shapes + [jax.ShapeDtypeStruct((4, 4 * rows, LANE), jnp.bfloat16)],
        compiler_params=pltpu.CompilerParams(vmem_limit_bytes=8 << 20),
        cost_estimate=pl.CostEstimate(flops=10**9, bytes_accessed=1 << 22, transcendentals=0),
        name="finish",
    )(head, body, *head_got, *body_got, *momenta)
    return outs[:4], outs[4:8], outs[8]


def by_corner(packed):
    return packed.reshape((-1, 4) + packed.shape[1:])


def newton_kernel(kind_ref, stack_ref, out_ref, gram_ref, rows_ref):
    kind = kind_ref[0]
    blocks, side, _ = stack_ref.shape
    chunk = out_ref.shape[1]
    tall = kind == 3
    paired = kind == 1

    @pl.when(tall)
    def _():
        total = dot(stack_ref[0], stack_ref[0], 0, 0)
        for block in range(1, blocks):
            total = total + dot(stack_ref[block], stack_ref[block], 0, 0)
        gram_ref[...] = total

    @pl.when(paired)
    def _():
        cross = dot(stack_ref[0], stack_ref[1], 1, 1)
        cross = cross + dot(stack_ref[1], stack_ref[0], 1, 1)
        gram_ref[...] = dot(stack_ref[0], stack_ref[0], 1, 1) + cross

    @pl.when(jnp.logical_not(jnp.logical_or(tall, paired)))
    def _():
        total = dot(stack_ref[0], stack_ref[0], 1, 1)
        for block in range(1, blocks):
            total = total + dot(stack_ref[block], stack_ref[block], 1, 1)
        gram_ref[...] = total

    row = lax.broadcasted_iota(jnp.int32, (side, side), 0)
    column = lax.broadcasted_iota(jnp.int32, (side, side), 1)
    eye = (row == column).astype(jnp.float32)
    gram = gram_ref[...]
    inverse = 1.0 / (jnp.sqrt(jnp.sum(gram * eye)) + 1e-07)
    gram_ref[...] = gram * (inverse * inverse)

    @pl.when(tall)
    def _():
        for block in range(blocks):
            rows_ref[block * chunk : (block + 1) * chunk] = stack_ref[block, :chunk].astype(jnp.float32) * inverse

    @pl.when(jnp.logical_not(tall))
    def _():
        rows_ref[...] = eye[: blocks * chunk] * inverse

    def halves(values):
        high = values.astype(jnp.bfloat16)
        return high, (values - high.astype(jnp.float32)).astype(jnp.bfloat16)

    def product(left, right):
        return dot(left[0], right[0]) + (dot(left[1], right[0]) + dot(left[0], right[1]))

    def mix(gram, parts):
        return halves(newton_first * eye + newton_second * gram + newton_third * product(parts, parts))

    def sweep(step, carry):
        gram = gram_ref[...]
        parts = halves(gram)
        mixer = mix(gram, parts)
        rows_ref[...] = product(halves(rows_ref[...]), mixer)
        gram_ref[...] = product(halves(product(parts, mixer)), mixer)
        return carry

    lax.fori_loop(0, 4, sweep, 0)
    gram = gram_ref[...]
    rows = product(halves(rows_ref[...]), mix(gram, halves(gram)))

    @pl.when(tall)
    def _():
        for block in range(blocks):
            out_ref[block] = rows[block * chunk : (block + 1) * chunk].astype(out_ref.dtype)

    @pl.when(jnp.logical_not(tall))
    def _():
        own = halves(rows[:chunk])
        first = dot(own[0], stack_ref[0]) + dot(own[1], stack_ref[0])
        second = dot(own[0], stack_ref[1])
        out_ref[0] = jnp.where(paired, first + second, first).astype(out_ref.dtype)
        out_ref[1] = (second + dot(own[1], stack_ref[1])).astype(out_ref.dtype)
        for block in range(2, blocks):
            out_ref[block] = (dot(own[0], stack_ref[block]) + dot(own[1], stack_ref[block])).astype(out_ref.dtype)


def newton_rows(stack, kind, chunk):
    blocks, side, lanes = stack.shape
    return pl.pallas_call(
        newton_kernel,
        out_shape=jax.ShapeDtypeStruct((blocks, chunk, lanes), jnp.bfloat16),
        in_specs=[
            pl.BlockSpec(memory_space=pltpu.SMEM),
            pl.BlockSpec(memory_space=pltpu.VMEM),
        ],
        out_specs=pl.BlockSpec(memory_space=pltpu.VMEM),
        scratch_shapes=[pltpu.VMEM((side, side), jnp.float32), pltpu.VMEM((blocks * chunk, side), jnp.float32)],
        compiler_params=pltpu.CompilerParams(vmem_limit_bytes=48 << 20),
        cost_estimate=pl.CostEstimate(flops=20 * 10**9, bytes_accessed=1 << 22, transcendentals=0),
        name="newton_rows",
    )(kind, stack)


def add_tree(values):
    while len(values) > 1:
        values = [left + right for left, right in zip(values[::2], values[1::2])]
    return values[0]


def collect(packed, small, rank, devices):
    planes = devices // CELL
    plane = rank // CELL
    rows = packed.shape[1]
    count = small.shape[0]

    def pair(values):
        high, low = split_wide(values)
        return jnp.concatenate([high, low])

    def value(sent):
        return join_wide(sent[:count], sent[count:])

    sent = pair(small)
    pieces, sums = [pick(packed, jnp.minimum(plane, MATRICES - 1), 0)], [value(sent)]
    for step in range(1, planes):
        give = pick(packed, jnp.minimum(plane ^ step, MATRICES - 1), 0)
        got = exchange(jnp.concatenate([give, sent]), devices, CELL * step)
        pieces.append(got[:rows])
        sums.append(value(got[rows:]))
    current = jnp.concatenate(pieces)
    total = add_tree(sums)
    for mask in (4, 2, 1):
        sent = pair(total)
        got = exchange(jnp.concatenate([current, sent]), devices, mask)
        length = current.shape[0]
        current = jnp.concatenate([current, got[:length]])
        total = value(sent) + value(got[length:])
    return current.reshape(CELL, planes, rows, LANE), total


PAD_TOK = 64
KEY_ROWS = 56
PAD_IMG = 256
GROUPS = 4
NEVER = -1e30
f32 = jnp.float32
bf16 = jnp.bfloat16


def window_matrix():
    table = np.zeros((PAD_IMG, PATCHES), np.float32)
    blocks = SIDE // WIN
    for window in range(blocks * blocks):
        for token in range(WIN_TOK):
            row = (window // blocks) * WIN + token // WIN
            column = (window % blocks) * WIN + token % WIN
            patch = ((row + SHIFT) % SIDE) * SIDE + (column + SHIFT) % SIDE
            table[window * PAD_TOK + token, patch] = 1.0
    return table


def dot(left, right, left_dim=1, right_dim=0):
    return lax.dot_general(
        left, right, (((left_dim,), (right_dim,)), ((), ())), preferred_element_type=jnp.float32
    )


def normalize(values):
    center = values - jnp.mean(values, axis=-1, keepdims=True)
    spread = jnp.mean(center * center, axis=-1, keepdims=True)
    factor = lax.rsqrt(spread + 1e-05)
    return center * factor, factor


def normalize_back(grad, gain, hat, factor):
    inner = grad * gain
    return factor * (
        inner
        - jnp.mean(inner, axis=-1, keepdims=True)
        - hat * jnp.mean(inner * hat, axis=-1, keepdims=True)
    )


def head_masks(dtype):
    lane = lax.broadcasted_iota(jnp.int32, (1, 128), 1) // 32
    return [(lane == head).astype(dtype) for head in range(GROUPS)]


def spread_heads(rows, masks):
    return jnp.concatenate([rows * mask for mask in masks], axis=0)


def fold_heads(blocks, masks):
    total = None
    for head, mask in enumerate(masks):
        part = blocks[head * PAD_TOK : (head + 1) * PAD_TOK] * mask
        total = part if total is None else total + part
    return total


def load_image(ref, image, slots):
    return jnp.concatenate([ref[lane, pl.ds(image, PATCHES, stride=slots), :] for lane in range(ref.shape[0])], axis=1)


def store_image(ref, image, slots, values):
    for lane in range(ref.shape[0]):
        ref[lane, pl.ds(image, PATCHES, stride=slots), :] = values[:, lane * 128 : (lane + 1) * 128]


def cut_lanes(ref, values):
    for lane in range(ref.shape[0]):
        ref[lane] = values[:, lane * 128 : (lane + 1) * 128]


def join_lanes(ref):
    return jnp.concatenate([ref[lane] for lane in range(ref.shape[0])], axis=1)


def attend_kernel(
    rank_ref, images_ref, gains_ref, shifts_ref, biases_ref, combined_ref, take_ref, put_ref, *refs, pieces, shard,
):
    windows_ref, triple_ref, attention_ref, mixed_ref, weights_ref, features_ref, scratch_ref = refs[pieces:]
    step = pl.program_id(0)
    width = images_ref.shape[-1]
    slots = images_ref.shape[0] // PATCHES
    scale = 1.0 / math.sqrt(width // HEADS)

    @pl.when(step == 0)
    def _():
        cut_lanes(features_ref, images_ref[...].astype(f32))
        if pieces > 1:
            place_rows(rank_ref[0], refs[:pieces], (weights_ref,), ((3, shard),))
        else:
            weights_ref[...] = refs[0][...]

    masks = head_masks(bf16)
    masks_wide = head_masks(f32)
    count = windows_ref.shape[0]
    for sub in range(count):
        image = step * count + sub
        features = load_image(features_ref, image, slots)
        hat, _ = normalize(features)
        normed = (hat * gains_ref[0:1] + shifts_ref[0:1]).astype(bf16)
        windows = dot(take_ref[...], normed).astype(bf16)
        windows_ref[sub] = windows
        for part in range(3):
            columns = slice(part * width, (part + 1) * width)
            values = dot(windows, weights_ref[part]) + biases_ref[0:1, columns]
            if part == 0:
                values = values * scale
            triple_ref[sub, :, columns] = values.astype(bf16)
        for window in range(4):
            rows = slice(window * PAD_TOK, (window + 1) * PAD_TOK)
            for group in range(GROUPS):
                lanes = slice(group * 128, (group + 1) * 128)
                query = triple_ref[sub, rows, group * 128 : (group + 1) * 128]
                key = triple_ref[sub, rows, width + group * 128 : width + (group + 1) * 128]
                value = triple_ref[sub, rows, 2 * width + group * 128 : 2 * width + (group + 1) * 128]
                scores = dot(key, spread_heads(query, masks), 1, 1)[:KEY_ROWS] + combined_ref[window, group]
                top = jnp.max(scores, axis=0, keepdims=True)
                raised = jnp.exp(scores - top)
                attention = raised * (1.0 / jnp.sum(raised, axis=0, keepdims=True))
                low = jnp.concatenate([attention, jnp.zeros((PAD_TOK - KEY_ROWS, attention.shape[1]), f32)], axis=0).astype(bf16)
                attention_ref[sub, window, group] = low
                out = dot(low, value, 0, 0)
                scratch_ref[sub, rows, lanes] = fold_heads(out, masks_wide).astype(bf16)
        store_image(mixed_ref, image, slots, dot(put_ref[...], scratch_ref[sub]))


def whole(shape):
    return pl.BlockSpec(shape, lambda i: (0,) * len(shape))


def one(shape, count=1):
    return pl.BlockSpec((count,) + shape, lambda i: (i,) + (0,) * len(shape))


def attend_forward(rank, sources, shard, images, gains, shifts, biases, combined, take, put):
    rows, width = images.shape
    slots = rows // PATCHES
    return pl.pallas_call(
        partial(attend_kernel, pieces=len(sources), shard=shard),
        grid=(slots // 2,),
        in_specs=[
            pl.BlockSpec(memory_space=pltpu.SMEM), whole(images.shape), whole(gains.shape), whole(shifts.shape),
            whole(biases.shape), whole(combined.shape), whole(take.shape), whole(put.shape),
        ]
        + [whole(source.shape) for source in sources],
        out_specs=[
            one((PAD_IMG, width), 2), one((PAD_IMG, 3 * width), 2), one((4, GROUPS, PAD_TOK, 256), 2),
            whole((width // 128, rows, 128)), whole((3, width, width)),
        ],
        out_shape=[
            jax.ShapeDtypeStruct((slots, PAD_IMG, width), bf16),
            jax.ShapeDtypeStruct((slots, PAD_IMG, 3 * width), bf16),
            jax.ShapeDtypeStruct((slots, 4, GROUPS, PAD_TOK, 256), bf16),
            jax.ShapeDtypeStruct((width // 128, rows, 128), f32),
            jax.ShapeDtypeStruct((3, width, width), bf16),
        ],
        scratch_shapes=[pltpu.VMEM((width // 128, rows, 128), f32), pltpu.VMEM((2, PAD_IMG, width), bf16)],
        compiler_params=pltpu.CompilerParams(vmem_limit_bytes=60 << 20),
        cost_estimate=pl.CostEstimate(flops=20*10**9, bytes_accessed=1 << 24, transcendentals=0),
        name="attend_forward",
    )(rank, images, gains, shifts, biases, combined, take, put, *sources)


def gelu_parts(values):
    size = jnp.abs(values) * math.sqrt(0.5)
    bell = jnp.exp(-0.5 * values * values)
    turn = 1.0 / (1.0 + 0.3275911 * size)
    tail = 1.061405429
    for factor in (-1.453152027, 1.421413741, -0.284496736, 0.254829592):
        tail = tail * turn + factor
    tail = 0.5 * tail * turn * bell
    share = jnp.where(values < 0.0, tail, 1.0 - tail)
    return share, values * bell * (1.0 / math.sqrt(2.0 * math.pi))


def feed_kernel(
    count_ref, rank_ref, images_ref, cotangent_ref, mixed_ref, gains_ref, shifts_ref, biases_ref, *refs, slots, shard, sources,
):
    block_ref, grad_middle_ref, grad_mixed_ref, sums_ref, hidden_sums_ref, *grad_refs = refs[sources:]
    merge_ref, expand_ref, project_ref = grad_refs[2:5] if shard else refs[:3]
    merge_grad_ref, expand_grad_ref, project_grad_ref = grad_refs[-3:]
    step = pl.program_id(0)
    rows, width = cotangent_ref.shape
    pieces, _, piece = expand_ref.shape
    hidden = pieces * piece
    @pl.when(step == 0)
    def _():
        project_grad_ref[...] = jnp.zeros_like(project_grad_ref)
        expand_grad_ref[...] = jnp.zeros_like(expand_grad_ref)
        merge_grad_ref[...] = jnp.zeros_like(merge_grad_ref)
        sums_ref[...] = jnp.zeros_like(sums_ref)
        hidden_sums_ref[...] = jnp.zeros_like(hidden_sums_ref)
        if shard:
            spans = ((1, shard), (pieces, shard), (1, project_ref.shape[1] // (width // shard)))
            place_rows(rank_ref[0], refs[:sources], (merge_ref, expand_ref, project_ref), spans)

    mixed = join_lanes(mixed_ref).astype(bf16)
    branch = dot(mixed, merge_ref[0]) + biases_ref[0:1, 3 * width : 4 * width]
    middle = images_ref[...].astype(f32) + branch
    slot = lax.broadcasted_iota(jnp.int32, (rows, 1), 0) % slots
    live = slot < count_ref[0]

    hat, factor = normalize(middle)
    gain = gains_ref[1:2]
    normed = (hat * gain + shifts_ref[1:2]).astype(bf16)
    grad_out = jnp.where(live, cotangent_ref[...].astype(f32), 0.0)
    grad_low = grad_out.astype(bf16)
    out = biases_ref[0:1, 4 * width + hidden : 5 * width + hidden]
    back = 0.0
    for index in range(pieces):
        columns = slice(index * piece, (index + 1) * piece)
        offset = 4 * width + index * piece
        pre = dot(normed, expand_ref[index]) + biases_ref[0:1, offset : offset + piece]
        share, slope = gelu_parts(pre)
        active = (pre * share).astype(bf16)
        out = out + dot(active, project_ref[0, columns])
        project_grad_ref[columns] += dot(active, grad_low, 0, 0)
        grad_pre = (dot(grad_low, project_ref[0, columns], 1, 1) * (share + slope)).astype(bf16)
        expand_grad_ref[index] += dot(normed, grad_pre, 0, 0)
        hidden_sums_ref[0:1, columns] += jnp.sum(grad_pre.astype(f32), axis=0, keepdims=True)
        back = back + dot(grad_pre, expand_ref[index], 1, 1)
    block_ref[...] = jnp.where(live, middle + out, 0.0).astype(bf16)
    grad_middle = grad_out + normalize_back(back, gain, hat, factor)
    cut_lanes(grad_middle_ref, grad_middle)
    grad_branch = grad_middle.astype(bf16)
    merge_grad_ref[...] += dot(mixed, grad_branch, 0, 0)
    cut_lanes(grad_mixed_ref, dot(grad_branch, merge_ref[0], 1, 1))
    sums_ref[0:1] += jnp.sum(back * hat, axis=0, keepdims=True)
    sums_ref[1:2] += jnp.sum(back, axis=0, keepdims=True)
    sums_ref[2:3] += jnp.sum(grad_out, axis=0, keepdims=True)
    sums_ref[3:4] += jnp.sum(grad_branch.astype(f32), axis=0, keepdims=True)
    if shard:

        @pl.when(step == pl.num_programs(0) - 1)
        def _():
            sources = ((merge_grad_ref, 1), (expand_grad_ref, pieces), (project_grad_ref, 1))
            store_core(sources, grad_refs[0], grad_refs[1], BODY, shard, rank_ref[0] & 1)


def feed_forward(count, rank, sources, hidden, images, cotangent, mixed, gains, shifts, biases, slots, tile, devices):
    rows, width = cotangent.shape
    expand_shape = (hidden // LANE, width, LANE)
    lanes = pl.BlockSpec((width // 128, tile, 128), lambda i: (0, i, 0))
    shard = width // devices
    raw = [(width, width), expand_shape, (hidden, width)]
    grad_shapes = [jax.ShapeDtypeStruct(shape, f32) for shape in raw]
    scratch = []
    if aligned(shard):
        grad_shapes = [
            jax.ShapeDtypeStruct((devices // 2, 9 * shard, width), f32),
            jax.ShapeDtypeStruct((devices // 2, 10 * shard, width), bf16),
        ]
        scratch = [pltpu.VMEM(shape, bf16) for shape in ((1, width, width), expand_shape, (1, hidden, width))]
        scratch += [pltpu.VMEM(shape, f32) for shape in raw]

    def tiled(columns):
        return pl.BlockSpec((tile, columns), lambda i: (i, 0))

    return pl.pallas_call(
        partial(feed_kernel, slots=slots, shard=shard if aligned(shard) else 0, sources=len(sources)),
        grid=(rows // tile,),
        in_specs=[
            pl.BlockSpec(memory_space=pltpu.SMEM), pl.BlockSpec(memory_space=pltpu.SMEM), tiled(width), tiled(width), lanes,
            whole(gains.shape), whole(shifts.shape), whole(biases.shape),
        ]
        + [whole(source.shape) for source in sources],
        out_specs=[tiled(width), lanes, lanes, whole((8, width)), whole((8, hidden))]
        + [whole(shape.shape) for shape in grad_shapes],
        out_shape=[
            jax.ShapeDtypeStruct((rows, width), bf16),
            jax.ShapeDtypeStruct((width // 128, rows, 128), f32),
            jax.ShapeDtypeStruct((width // 128, rows, 128), f32),
            jax.ShapeDtypeStruct((8, width), f32),
            jax.ShapeDtypeStruct((8, hidden), f32),
        ]
        + grad_shapes,
        scratch_shapes=scratch,
        compiler_params=pltpu.CompilerParams(vmem_limit_bytes=60 << 20),
        cost_estimate=pl.CostEstimate(flops=44*10**9, bytes_accessed=1 << 24, transcendentals=0),
        name="feed_forward",
    )(count, rank, images, cotangent, mixed, gains, shifts, biases, *sources)


def attend_back_kernel(
    mine_ref, grad_mixed_ref, triple_ref, attention_ref, windows_ref, take_ref,
    grad_triple_ref, table_ref, sums_ref, *grad_refs, shard,
):
    attend_grad_ref = grad_refs[-1]
    step = pl.program_id(0)
    width = windows_ref.shape[-1]
    slots = grad_mixed_ref.shape[1] // PATCHES
    scale = 1.0 / math.sqrt(width // HEADS)

    @pl.when(step == 0)
    def _():
        attend_grad_ref[...] = jnp.zeros_like(attend_grad_ref)
        table_ref[...] = jnp.zeros_like(table_ref)
        sums_ref[...] = jnp.zeros_like(sums_ref)

    grad_mixed = dot(take_ref[...], load_image(grad_mixed_ref, step, slots).astype(bf16)).astype(bf16)
    masks = head_masks(bf16)
    masks_wide = head_masks(f32)
    pad = jnp.zeros((PAD_TOK - KEY_ROWS, 256), f32)
    for group in range(GROUPS):
        table = table_ref[group]
        for window in range(4):
            rows = slice(window * PAD_TOK, (window + 1) * PAD_TOK)
            query = triple_ref[0, rows, group * 128 : (group + 1) * 128]
            key = triple_ref[0, rows, width + group * 128 : width + (group + 1) * 128]
            value = triple_ref[0, rows, 2 * width + group * 128 : 2 * width + (group + 1) * 128]
            grad_heads = spread_heads(grad_mixed[rows, group * 128 : (group + 1) * 128], masks)
            attention_low = attention_ref[0, window, group]
            attention = attention_low.astype(f32)[:KEY_ROWS]
            grad_attention = dot(value, grad_heads, 1, 1)[:KEY_ROWS]
            inner = jnp.sum(grad_attention * attention, axis=0, keepdims=True)
            grad_scores = attention * (grad_attention - inner)
            low = jnp.concatenate([grad_scores, pad], axis=0).astype(bf16)
            table = table + low.astype(f32)[:KEY_ROWS]
            grad_value = dot(attention_low, grad_heads)
            grad_key = dot(low, spread_heads(query, masks))
            grad_query = fold_heads(dot(low, key, 0, 0), masks_wide) * scale
            grad_triple_ref[0, rows, group * 128 : (group + 1) * 128] = grad_query.astype(bf16)
            grad_triple_ref[0, rows, width + group * 128 : width + (group + 1) * 128] = grad_key.astype(bf16)
            grad_triple_ref[0, rows, 2 * width + group * 128 : 2 * width + (group + 1) * 128] = grad_value.astype(bf16)
        table_ref[group] = table
    for part in range(3):
        columns = slice(part * width, (part + 1) * width)
        grad = grad_triple_ref[0, :, columns]
        attend_grad_ref[part] += dot(windows_ref[0], grad, 0, 0)
        sums_ref[0:1, columns] += jnp.sum(grad.astype(f32), axis=0, keepdims=True)
    if shard:

        @pl.when(step == pl.num_programs(0) - 1)
        def _():
            store_core(((attend_grad_ref, 3),), grad_refs[0], grad_refs[1], HEAD, shard, mine_ref[0])


def attend_backward(mine, devices, grad_mixed, triple, attention, windows, take):
    width = windows.shape[-1]
    slots = triple.shape[0]
    shard = width // devices
    grad_shapes, scratch = [jax.ShapeDtypeStruct((3, width, width), f32)], []
    if aligned(shard):
        grad_shapes = [
            jax.ShapeDtypeStruct((devices // 2, 3 * shard, width), f32),
            jax.ShapeDtypeStruct((devices // 2, 3 * shard, width), bf16),
        ]
        scratch = [pltpu.VMEM((3, width, width), f32)]
    return pl.pallas_call(
        partial(attend_back_kernel, shard=shard if aligned(shard) else 0),
        grid=(slots,),
        in_specs=[
            pl.BlockSpec(memory_space=pltpu.SMEM), whole(grad_mixed.shape), one((PAD_IMG, 3 * width)),
            one((4, GROUPS, PAD_TOK, 256)), one((PAD_IMG, width)), whole(take.shape),
        ],
        out_specs=[one((PAD_IMG, 3 * width)), whole((GROUPS, KEY_ROWS, 256)), whole((8, 3 * width))]
        + [whole(shape.shape) for shape in grad_shapes],
        out_shape=[
            jax.ShapeDtypeStruct((slots, PAD_IMG, 3 * width), bf16),
            jax.ShapeDtypeStruct((GROUPS, KEY_ROWS, 256), f32),
            jax.ShapeDtypeStruct((8, 3 * width), f32),
        ]
        + grad_shapes,
        scratch_shapes=scratch,
        compiler_params=pltpu.CompilerParams(vmem_limit_bytes=60 << 20),
        cost_estimate=pl.CostEstimate(flops=37*10**9, bytes_accessed=1 << 24, transcendentals=0),
        name="attend_backward",
    )(mine, grad_mixed, triple, attention, windows, take)


def input_kernel(images_ref, grad_triple_ref, grad_middle_ref, weights_ref, gains_ref, put_ref, out_ref, sums_ref, features_ref, grads_ref):
    step = pl.program_id(0)
    width = images_ref.shape[-1]
    slots = images_ref.shape[0] // PATCHES

    @pl.when(step == 0)
    def _():
        sums_ref[...] = jnp.zeros_like(sums_ref)
        cut_lanes(features_ref, images_ref[...].astype(f32))

    for sub in range(grad_triple_ref.shape[0]):
        image = step * grad_triple_ref.shape[0] + sub
        hat, factor = normalize(load_image(features_ref, image, slots))
        grad = 0.0
        for part in range(3):
            grad = grad + dot(grad_triple_ref[sub, :, part * width : (part + 1) * width], weights_ref[part], 1, 1)
        high = grad.astype(bf16)
        low = (grad - high.astype(f32)).astype(bf16)
        grad = dot(put_ref[...], high) + dot(put_ref[...], low)
        total = load_image(grad_middle_ref, image, slots) + normalize_back(grad, gains_ref[0:1], hat, factor)
        store_image(grads_ref, image, slots, total)
        sums_ref[0:1] += jnp.sum(grad * hat, axis=0, keepdims=True)
        sums_ref[1:2] += jnp.sum(grad, axis=0, keepdims=True)

    @pl.when(step == pl.num_programs(0) - 1)
    def _():
        out_ref[...] = join_lanes(grads_ref)


def input_backward(images, grad_triple, grad_middle, weights, gains, put):
    rows, width = images.shape
    slots = rows // PATCHES
    return pl.pallas_call(
        input_kernel,
        grid=(slots // 2,),
        in_specs=[
            whole((rows, width)), one((PAD_IMG, 3 * width), 2), whole(grad_middle.shape),
            pl.BlockSpec((3, width, width), lambda i: (0, 0, 0)), whole(gains.shape), whole(put.shape),
        ],
        out_specs=[whole((rows, width)), whole((8, width))],
        out_shape=[
            jax.ShapeDtypeStruct((rows, width), f32),
            jax.ShapeDtypeStruct((8, width), f32),
        ],
        scratch_shapes=[pltpu.VMEM((width // 128, rows, 128), f32)] * 2,
        compiler_params=pltpu.CompilerParams(vmem_limit_bytes=60 << 20),
        cost_estimate=pl.CostEstimate(flops=14*10**9, bytes_accessed=1 << 24, transcendentals=0),
        name="input_backward",
    )(images, grad_triple, grad_middle, weights, gains, put)


def combine_bias(bias_table, rel_index, shift_mask):
    one_hot = (rel_index.reshape(-1)[:, None] == jnp.arange(TABLE)[None, :]).astype(f32)
    position = jnp.dot(one_hot, bias_table, precision=lax.Precision.HIGHEST).T
    position = position.reshape(GROUPS, 4, WIN_TOK, WIN_TOK)
    position = jnp.transpose(position, (0, 3, 1, 2))
    position = jnp.pad(
        position, ((0, 0), (0, KEY_ROWS - WIN_TOK), (0, 0), (0, PAD_TOK - WIN_TOK))
    ).reshape(GROUPS, KEY_ROWS, 256)
    mask = jnp.transpose(-100.0 * (1 - shift_mask).astype(f32), (0, 2, 1))
    mask = jnp.pad(mask, ((0, 0), (0, 0), (0, PAD_TOK - WIN_TOK)))
    mask = jnp.pad(mask, ((0, 0), (0, KEY_ROWS - WIN_TOK), (0, 0)), constant_values=NEVER)
    mask = jnp.tile(mask, (1, 1, 4))
    return position[None] + mask[:, None], one_hot


def table_gradient(table, one_hot):
    grad = table.reshape(GROUPS, KEY_ROWS, 4, PAD_TOK)[:, :WIN_TOK, :, :WIN_TOK]
    grad = jnp.transpose(grad, (3, 1, 0, 2)).reshape(WIN_TOK * WIN_TOK, HEADS)
    return jnp.dot(one_hot.T, grad, precision=lax.Precision.HIGHEST)


def flat_rows(images):
    return jnp.transpose(images, (1, 0, 2)).reshape(-1, images.shape[-1])


def image_form(rows, slots):
    return jnp.transpose(rows.reshape(-1, slots, rows.shape[-1]), (1, 0, 2))


def adamw_step(param, grad, first, second, steps):
    first_next = 0.9 * first + 0.1 * grad
    second_next = 0.999 * second + 0.001 * grad * grad
    first_hat = first_next / (1.0 - jnp.power(0.9, steps))
    second_hat = second_next / (1.0 - jnp.power(0.999, steps))
    update = -0.05 * (first_hat / (jnp.sqrt(second_hat) + 1e-08) + 0.05 * param)
    return (first_next, second_next, update)


def column_blocks(matrix):
    rows, columns = matrix.shape
    return jnp.transpose(matrix.reshape(rows, columns // LANE, LANE), (1, 0, 2))


def from_blocks(blocks):
    count, rows, lanes = blocks.shape
    return jnp.transpose(blocks, (1, 0, 2)).reshape(rows, count * lanes)


def local(
    images,
    cotangent,
    image_counts,
    shift_mask,
    rel_index,
    step_count,
    attend_weight,
    merge_weight,
    expand_weight,
    project_weight,
    norm_gains,
    norm_shifts,
    layer_biases,
    bias_table,
    attend_momentum,
    merge_momentum,
    expand_momentum,
    project_momentum,
    gains_mean,
    gains_square,
    shifts_mean,
    shifts_square,
    biases_mean,
    biases_square,
    table_mean,
    table_square,
):
    slots, patches, width = images.shape
    devices = lax.axis_size("dp")
    hidden_units = expand_weight.shape[1]
    grad_scale = 1.0 / math.sqrt(slots * devices * PATCHES)
    rank = lax.axis_index("dp")
    planes = devices // CELL
    plane = rank // CELL
    corner = (rank // 2) % 4
    shard = width // devices
    tall_shard = hidden_units // devices

    attend_rows = column_blocks(attend_weight).reshape(-1, LANE)
    other_rows = jnp.concatenate(
        [column_blocks(merge_weight).reshape(-1, LANE), column_blocks(expand_weight).reshape(-1, LANE), project_weight]
    )
    near = gather_planes(attend_rows, devices)
    near[0], other_rows = lax.optimization_barrier((near[0], other_rows))
    other_near = gather_planes(other_rows, devices)
    near = gather_corners(jnp.stack(near), devices)
    near[0], other_near[1] = lax.optimization_barrier((near[0], other_near[1]))
    far = [exchange(piece, devices, 1) for piece in near]
    far[0], *other_near = lax.optimization_barrier((far[0], *other_near))
    other_near = gather_corners(jnp.stack(other_near), devices)
    other_far = [exchange(other_near[0], devices, 1)]
    attend_sources = near + far
    if not aligned(shard):
        attend_sources = order_rows(attend_sources, ((3, shard),), rank, devices)
    this = rank.reshape(1)

    take = jnp.asarray(window_matrix(), bf16)
    put = jnp.asarray(window_matrix().T, bf16)
    combined, one_hot = combine_bias(bias_table, rel_index, shift_mask)
    bias_row = layer_biases.reshape(1, -1)
    rows = flat_rows(images)
    windows, triple, attention, mixed, weights = attend_forward(
        this, attend_sources, shard, rows, norm_gains, norm_shifts, bias_row, combined, take, put
    )
    mixed, *arrived = lax.optimization_barrier((mixed, *other_near[1:]))
    other_far += [exchange(piece, devices, 1) for piece in arrived]
    sources = other_near[:1] + arrived + other_far
    if not aligned(shard):
        sources = order_rows(
            sources, ((1, shard), (hidden_units // LANE, shard), (1, tall_shard)), rank, devices
        )
    mine = (rank & 1).reshape(1)
    block_rows, grad_middle, grad_mixed, feed_sums, hidden_sums, *body_grads = feed_forward(
        image_counts, this, sources, hidden_units, rows, flat_rows(cotangent), mixed, norm_gains, norm_shifts, bias_row,
        slots, slots * patches // 4, devices,
    )
    block_out = image_form(block_rows, slots)
    if not aligned(shard):
        merge_term, expand_term, project_term = body_grads
        body_grads = pack_core([merge_term[None], expand_term, project_term[None]], BODY, shard, rank & 1)
    body_keep, body_sent = body_grads
    body_got = exchange(body_sent, devices, 1)
    body_own, body_sends = fold(by_corner(body_keep), [by_corner(body_got)], corner, BODY, shard)
    grad_mixed, *body_sends = lax.optimization_barrier((grad_mixed, *body_sends))
    body_got = send_all(body_sends, 2, devices)

    grad_triple, table_sums, triple_sums, *head_grads = attend_backward(
        mine, devices, grad_mixed, triple, attention, windows, take
    )
    if not aligned(shard):
        head_grads = pack_core(head_grads, HEAD, shard, rank & 1)
    head_keep, head_sent = head_grads
    head_got = exchange(head_sent, devices, 1)
    head_own, head_sends = fold(by_corner(head_keep), [by_corner(head_got)], corner, HEAD, shard)
    body_own, body_sends = fold(body_own[None], [got[None] for got in body_got], plane, BODY, shard)
    grad_triple, *sends = lax.optimization_barrier((grad_triple, *head_sends, *body_sends))
    head_got = send_all(sends[:3], 2, devices)
    body_got = send_all(sends[3:], CELL, devices)
    grad_triple, head_got[1] = lax.optimization_barrier((grad_triple, head_got[1]))
    input_rows, input_sums = input_backward(rows, grad_triple, grad_middle, weights, norm_gains, put)
    input_sums, head_got[0], head_got[2], *body_got = lax.optimization_barrier(
        (input_sums, head_got[0], head_got[2], *body_got)
    )
    input_grad = image_form(input_rows, slots)
    table_term = table_gradient(table_sums, one_hot)
    head_own, head_sends = fold(head_own[None], [got[None] for got in head_got], plane, HEAD, shard)
    head_got = send_all(head_sends, CELL, devices)
    momenta = (attend_momentum, merge_momentum, expand_momentum, project_momentum)
    grads, following, packed = finish(head_own, head_got, body_own, body_got, momenta, shard, grad_scale)

    small_parts = (
        jnp.stack([input_sums[0], feed_sums[0]]),
        jnp.stack([input_sums[1], feed_sums[1]]),
        jnp.concatenate([triple_sums[0], feed_sums[3], hidden_sums[0], feed_sums[2]]),
        table_term,
    )
    small = jnp.concatenate([part.reshape(-1) for part in small_parts])
    small = jnp.pad(small, (0, -small.shape[0] % (8 * LANE))).reshape(-1, LANE)

    length = tall_shard
    whole_rows, small = collect(packed, small, rank, devices)
    stack = whole_rows.reshape(CELL * planes, MATRICES, -1, LANE)
    stack = jnp.transpose(stack, (1, 0, 2, 3)).reshape(MATRICES, -1, LANE)
    kind = jnp.minimum(plane, MATRICES - 1).astype(jnp.int32).reshape(1)
    chunk = planes * length // MATRICES
    orth = newton_rows(stack, kind, chunk).reshape(MATRICES, planes, -1, LANE)
    pieces = [orth[:, 0]]
    for step in range(1, planes):
        pieces.append(exchange(orth[:, step], devices, CELL * step))
    received = jnp.stack(pieces)

    flat, start, small_sums = small.reshape(-1), 0, []
    for part in small_parts:
        small_sums.append(flat[start : start + part.size].reshape(part.shape))
        start += part.size
    small_grads = tuple((term * grad_scale for term in small_sums))
    results = [block_out, input_grad]
    for order, (grad, moment_next) in enumerate(zip(grads, following)):
        piece = pick(received, plane ^ order, 0)
        blocks = grad.shape[1] // LANE
        piece = piece.reshape(-1, LANE)[: blocks * grad.shape[0]].reshape(blocks, -1, LANE)
        extent = max(devices * grad.shape[0], grad.shape[1])
        update = -0.02 * math.sqrt(extent) * from_blocks(piece).astype(f32)
        results += [grad, moment_next, update]
    steps = step_count[0].astype(f32)
    params = (norm_gains, norm_shifts, layer_biases, bias_table)
    states = (
        (gains_mean, gains_square),
        (shifts_mean, shifts_square),
        (biases_mean, biases_square),
        (table_mean, table_square),
    )
    for param, grad, state in zip(params, small_grads, states):
        first_next, second_next, update = adamw_step(param, grad, state[0], state[1], steps)
        results += [grad, first_next, second_next, update]
    return tuple(results)


def solution(mesh):
    return jax.shard_map(
        local,
        mesh=mesh,
        in_specs=(
            P("dp", None, None),
            P("dp", None, None),
            P("dp"),
            P(),
            P(),
            P(),
            P("dp", None),
            P("dp", None),
            P("dp", None),
            P("dp", None),
            P(),
            P(),
            P(),
            P(),
            P("dp", None),
            P("dp", None),
            P("dp", None),
            P("dp", None),
            P(),
            P(),
            P(),
            P(),
            P(),
            P(),
            P(),
            P(),
        ),
        out_specs=(
            P("dp", None, None),
            P("dp", None, None),
            P("dp", None),
            P("dp", None),
            P("dp", None),
            P("dp", None),
            P("dp", None),
            P("dp", None),
            P("dp", None),
            P("dp", None),
            P("dp", None),
            P("dp", None),
            P("dp", None),
            P("dp", None),
            P(),
            P(),
            P(),
            P(),
            P(),
            P(),
            P(),
            P(),
            P(),
            P(),
            P(),
            P(),
            P(),
            P(),
            P(),
            P(),
        ),
        check_vma=False,
    )
```

profile of v0, /device:TPU:0, one launch (start us, length us, event | category | flops | bytes accessed | tf_op | source)
XLA Modules:
  0.0 266.4 jit_solution(2263828114519190549)
XLA Ops:
  1.5 3.1 %collective-permute-start = (bf16[48,512]{1,0:T(8,128)(2,1)S(1)}, bf16[48,512]{1,0:T(8,128)(2,1)S(1)}, u32[]{:S(2)}, u32[]{:S(2)}) collective-permute-start(bf16[48,512]{1,0:T(8,128)(2,1)S(1)} %bitcast.140), channel_id=1, source_target_pairs={{0,8},{1,9},{2,10},{3,11},{4,12},{5,13},{6,14},{7,15},{8,0},{9,1},... | collective-permute-start | bytes 147464 | tf_op jit(solution)/shard_map/ppermute | solution.py:32
  4.6 2.6 collective-permute-start.1
  9.9 3.5 %collective-permute-start.8 = (bf16[144,512]{1,0:T(8,128)(2,1)S(1)}, bf16[144,512]{1,0:T(8,128)(2,1)S(1)}, u32[]{:S(2)}, u32[]{:S(2)}) collective-permute-start(bf16[144,512]{1,0:T(8,128)(2,1)S(1)} %pad_maximum_fusion.9), channel_id=1, source_target_pairs={{0,16},{1,17},{2,18},{3,19},{4,20},{5,21},{6,22},{7,23},{8,24},{9,... | collective-permute-start | bytes 442376 | tf_op jit(solution)/shard_map/ppermute | solution.py:32
  15.2 1.6 collective-permute-start.4
  16.8 1.5 collective-permute-start.5
  18.8 2.0 convolution_bitcast_fusion
  22.9 3.3 %collective-permute-done.5.refs_2_ = bf16[4,48,512]{2,1,0:T(8,128)(2,1)S(1)} collective-permute-done((bf16[4,48,512]{2,1,0:T(8,128)(2,1)S(1)}, bf16[4,48,512]{2,1,0:T(8,128)(2,1)S(1)}, u32[]{:S(2)}, u32[]{:S(2)}) %collective-permute-start.5) | collective-permute-done | bytes 196640 | tf_op jit(solution)/shard_map/ppermute | solution.py:32
  28.9 1.6 collective-permute-start.13
  30.4 1.5 collective-permute-start.14
  32.6 19.9 %attend_forward.1 = (bf16[8,256,512]{2,1,0:T(8,128)(2,1)}, bf16[8,256,1536]{2,1,0:T(8,128)(2,1)}, bf16[8,4,4,64,256]{4,3,2,1,0:T(8,128)(2,1)}, f32[4,1568,128]{2,1,0:T(8,128)}, bf16[3,512,512]{2,1,0:T(8,128)(2,1)}) custom-call(s32[1]{0:T(128)} %bitcast.rank_ref, bf16[1568,512]{1,0:T(8,128)(2,1)} %bitcast.163, f32[2,512]{1,0:T(2,128)} %gains_ref.5, ...), custom_call_target="tpu_custom_call" | custom-call | flops 20000000000 | bytes 16777216 | tf_op jit(solution)/shard_map/attend_forward/pallas_call | solution.py:525
  52.6 4.6 %collective-permute-done.15.refs_3_ = bf16[4,144,512]{2,1,0:T(8,128)(2,1)S(1)} collective-permute-done((bf16[4,144,512]{2,1,0:T(8,128)(2,1)S(1)}, bf16[4,144,512]{2,1,0:T(8,128)(2,1)S(1)}, u32[]{:S(2)}, u32[]{:S(2)}) %collective-permute-start.15) | collective-permute-done | bytes 589856 | tf_op jit(solution)/shard_map/ppermute | solution.py:32
  61.7 47.8 %feed_forward.1 = (bf16[1568,512]{1,0:T(8,128)(2,1)}, f32[4,1568,128]{2,1,0:T(8,128)}, f32[4,1568,128]{2,1,0:T(8,128)}, f32[8,512]{1,0:T(8,128)}, f32[8,2048]{1,...) custom-call(s32[1]{0:T(128)S(6)} %copy.148.count_ref, s32[1]{0:T(128)} %bitcast.rank_ref, ...), custom_call_target="tpu_custom_call" | custom-call | flops 44000002048 | bytes 16777216 | tf_op jit(solution)/shard_map/feed_forward/pallas_call | solution.py:646
  109.8 5.0 %collective-permute-done.20 = bf16[16,160,512]{2,1,0:T(8,128)(2,1)S(1)} collective-permute-done((bf16[16,160,512]{2,1,0:T(8,128)(2,1)}, bf16[16,160,512]{2,1,0:T(8,128)(2,1)S(1)}, u32[]{:S(2)}, u32[]{:S(2)}) %collective-permute-start.20) | collective-permute-done | bytes 2621472 | tf_op jit(solution)/shard_map/ppermute | solution.py:32
  114.7 2.3 copy-done.4
  117.1 1.8 fold.4
  123.4 35.4 %attend_backward.1 = (bf16[8,256,1536]{2,1,0:T(8,128)(2,1)}, f32[4,56,256]{2,1,0:T(8,128)}, f32[8,1536]{1,0:T(8,128)}, f32[16,48,512]{2,1,0:T(8,128)}, bf16[16,48,512]{2,1,0:T(8,128)(2,1)}) custom-call(s32[1]{0:T(128)} %bitcast.24.mine_ref, f32[4,1568,128]{2,1,0:T(8,128)} %get-tuple-element.127.grad_mixed_ref, ...), custom_call_target="tpu_custom_call" | custom-call | flops 36999999488 | bytes 16777216 | tf_op jit(solution)/shard_map/attend_backward/pallas_call | solution.py:736
  164.2 1.5 fold.6
  166.9 1.9 fusion.1
  169.7 1.6 collective-permute-start.26
  173.6 3.3 %collective-permute-start.30 = (bf16[1,160,512]{2,1,0:T(8,128)(2,1)S(1)}, bf16[1,160,512]{2,1,0:T(8,128)(2,1)S(1)}, u32[]{:S(2)}, u32[]{:S(2)}) collective-permute-start(bf16[1,160,512]{2,1,0:T(8,128)(2,1)S(1)} %get-tuple-element.156), channel_id=1, source_target_pairs={{0,24},{1,25},{2,26},{3,27},{4,28},{5,29},{6,30},{7,31},{8,16},{9,... | collective-permute-start | bytes 491528 | tf_op jit(solution)/shard_map/ppermute | solution.py:32
  176.9 13.8 %input_backward.1 = (f32[1568,512]{1,0:T(8,128)}, f32[8,512]{1,0:T(8,128)}) custom-call(bf16[1568,512]{1,0:T(8,128)(2,1)} %bitcast.165, bf16[8,256,1536]{2,1,0:T(8,128)(2,1)} %get-tuple-element.146.grad_triple_ref, f32[4,1568,128]{2,1,0:T(8,128)} %get-tuple-element.147.grad_middle_ref, bf16[3,512,512]{2,1,0:T(8,128)(2,1)} %get-tuple-element.148.weights_ref, ...), custom_call_target="tpu_custom_call" | custom-call | flops 14000000000 | bytes 16777216 | tf_op jit(solution)/shard_map/input_backward/pallas_call | solution.py:790
  193.0 3.3 %collective-permute-start.33 = (bf16[1,48,512]{2,1,0:T(8,128)(2,1)S(1)}, bf16[1,48,512]{2,1,0:T(8,128)(2,1)S(1)}, u32[]{:S(2)}, u32[]{:S(2)}) collective-permute-start(bf16[1,48,512]{2,1,0:T(8,128)(2,1)S(1)} %get-tuple-element.164), channel_id=1, source_target_pairs={{0,24},{1,25},{2,26},{3,27},{4,28},{5,29},{6,30},{7,31},{8,16},{9,... | collective-permute-start | bytes 147464 | tf_op jit(solution)/shard_map/ppermute | solution.py:32
  197.1 1.9 collective-permute-done.33.refs_4_
  200.0 4.0 %collective-permute-start.35 = (bf16[112,512]{1,0:T(8,128)(2,1)S(1)}, bf16[112,512]{1,0:T(8,128)(2,1)S(1)}, u32[]{:S(2)}, u32[]{:S(2)}) collective-permute-start(bf16[112,512]{1,0:T(8,128)(2,1)S(1)} %get-tuple-element.275), channel_id=1, source_target_pairs={{0,16},{1,17},{2,18},{3,19},{4,20},{5,21},{6,22},{7,23},{8,24},{9,... | collective-permute-start | bytes 344072 | tf_op jit(solution)/shard_map/ppermute | solution.py:32
  206.0 2.8 %collective-permute-done.35 = bf16[112,512]{1,0:T(8,128)(2,1)S(1)} collective-permute-done((bf16[112,512]{1,0:T(8,128)(2,1)S(1)}, bf16[112,512]{1,0:T(8,128)(2,1)S(1)}, u32[]{:S(2)}, u32[]{:S(2)}) %collective-permute-start.35) | collective-permute-done | bytes 114720 | tf_op jit(solution)/shard_map/ppermute | solution.py:32
  212.1 6.2 %collective-permute-done.37 = bf16[304,512]{1,0:T(8,128)(2,1)S(1)} collective-permute-done((bf16[304,512]{1,0:T(8,128)(2,1)S(1)}, bf16[304,512]{1,0:T(8,128)(2,1)S(1)}, u32[]{:S(2)}, u32[]{:S(2)}) %collective-permute-start.37) | collective-permute-done | bytes 311328 | tf_op jit(solution)/shard_map/ppermute | solution.py:32
  220.4 8.6 %collective-permute-done.38 = bf16[560,512]{1,0:T(8,128)(2,1)S(1)} collective-permute-done((bf16[560,512]{1,0:T(8,128)(2,1)S(1)}, bf16[560,512]{1,0:T(8,128)(2,1)S(1)}, u32[]{:S(2)}, u32[]{:S(2)}) %collective-permute-start.38) | collective-permute-done | bytes 573472 | tf_op jit(solution)/shard_map/ppermute | solution.py:32
  231.9 2.2 collective-permute-done.39
  236.5 17.4 %newton_rows.1 = bf16[4,64,512]{2,1,0:T(8,128)(2,1)S(1)} custom-call(s32[1]{0:T(128)} %bitcast.41.kind_ref, bf16[4,512,512]{2,1,0:T(8,128)(2,1)S(1)} %bitcast.120), custom_call_target="tpu_custom_call" | custom-call | flops 20000000000 | bytes 4194304 | tf_op jit(solution)/shard_map/newton_rows/pallas_call | solution.py:333
  255.2 2.1 collective-permute-start.41
  257.4 1.4 collective-permute-start.42
  260.8 3.0 %collective-permute-done.42 = bf16[4,16,512]{2,1,0:T(8,128)(2,1)S(1)} collective-permute-done((bf16[4,16,512]{2,1,0:T(8,128)(2,1)S(1)}, bf16[4,16,512]{2,1,0:T(8,128)(2,1)S(1)}, u32[]{:S(2)}, u32[]{:S(2)}) %collective-permute-start.42) | collective-permute-done | bytes 65568 | tf_op jit(solution)/shard_map/ppermute | solution.py:32
  (212 shorter events, 51.0 us)
Async XLA Ops:
  1.5 13.6 %collective-permute-start = (bf16[48,512]{1,0:T(8,128)(2,1)S(1)}, bf16[48,512]{1,0:T(8,128)(2,1)S(1)}, u32[]{:S(2)}, u32[]{:S(2)}) collective-permute-start(bf16[48,512]{1,0:T(8,128)(2,1)S(1)} %bitcast.140), channel_id=1, source_target_pairs={{0,8},{1,9},{2,10},{3,11},{4,12},{5,13},{6,14},{7,15},{8,0},{9,1},... | collective-permute-start | bytes 147464 | tf_op jit(solution)/shard_map/ppermute | solution.py:32
  4.6 10.5 %collective-permute-start.1 = (bf16[48,512]{1,0:T(8,128)(2,1)S(1)}, bf16[48,512]{1,0:T(8,128)(2,1)S(1)}, u32[]{:S(2)}, u32[]{:S(2)}) collective-permute-start(bf16[48,512]{1,0:T(8,128)(2,1)S(1)} %bitcast.141), channel_id=1, source_target_pairs={{0,16},{1,17},{2,18},{3,19},{4,20},{5,21},{6,22},{7,23},{8,24},{9,... | collective-permute-start | bytes 147464 | tf_op jit(solution)/shard_map/ppermute | solution.py:32
  7.2 8.0 %collective-permute-start.2 = (bf16[48,512]{1,0:T(8,128)(2,1)S(1)}, bf16[48,512]{1,0:T(8,128)(2,1)S(1)}, u32[]{:S(2)}, u32[]{:S(2)}) collective-permute-start(bf16[48,512]{1,0:T(8,128)(2,1)S(1)} %bitcast.142), channel_id=1, source_target_pairs={{0,24},{1,25},{2,26},{3,27},{4,28},{5,29},{6,30},{7,31},{8,16},{9,... | collective-permute-start | bytes 147464 | tf_op jit(solution)/shard_map/ppermute | solution.py:32
  8.9 12.8 %collective-permute-start.3 = (bf16[144,512]{1,0:T(8,128)(2,1)S(1)}, bf16[144,512]{1,0:T(8,128)(2,1)S(1)}, u32[]{:S(2)}, u32[]{:S(2)}) collective-permute-start(bf16[144,512]{1,0:T(8,128)(2,1)S(1)} %pad_maximum_fusion.9), channel_id=1, source_target_pairs={{0,8},{1,9},{2,10},{3,11},{4,12},{5,13},{6,14},{7,15},{8,0},{9,1},... | collective-permute-start | bytes 442376 | tf_op jit(solution)/shard_map/ppermute | solution.py:32
  9.9 12.0 %collective-permute-start.8 = (bf16[144,512]{1,0:T(8,128)(2,1)S(1)}, bf16[144,512]{1,0:T(8,128)(2,1)S(1)}, u32[]{:S(2)}, u32[]{:S(2)}) collective-permute-start(bf16[144,512]{1,0:T(8,128)(2,1)S(1)} %pad_maximum_fusion.9), channel_id=1, source_target_pairs={{0,16},{1,17},{2,18},{3,19},{4,20},{5,21},{6,22},{7,23},{8,24},{9,... | collective-permute-start | bytes 442376 | tf_op jit(solution)/shard_map/ppermute | solution.py:32
  15.2 7.7 %collective-permute-start.4 = (bf16[4,48,512]{2,1,0:T(8,128)(2,1)S(1)}, bf16[4,48,512]{2,1,0:T(8,128)(2,1)S(1)}, u32[]{:S(2)}, u32[]{:S(2)}) collective-permute-start(bf16[4,48,512]{2,1,0:T(8,128)(2,1)S(1)} %pad_maximum_fusion.2.refs_0_), channel_id=1, source_target_pairs={{0,2},{1,3},{2,0},{3,1},{4,6},{5,7},{6,4},{7,5},{8,10},{9,11},{10,... | collective-permute-start | bytes 589832 | tf_op jit(solution)/shard_map/ppermute | solution.py:32
  16.8 9.5 %collective-permute-start.5 = (bf16[4,48,512]{2,1,0:T(8,128)(2,1)S(1)}, bf16[4,48,512]{2,1,0:T(8,128)(2,1)S(1)}, u32[]{:S(2)}, u32[]{:S(2)}) collective-permute-start(bf16[4,48,512]{2,1,0:T(8,128)(2,1)S(1)} %pad_maximum_fusion.2.refs_0_), channel_id=1, source_target_pairs={{0,4},{1,5},{2,6},{3,7},{4,0},{5,1},{6,2},{7,3},{8,12},{9,13},{10,... | collective-permute-start | bytes 589832 | tf_op jit(solution)/shard_map/ppermute | solution.py:32
  18.3 8.0 %collective-permute-start.6 = (bf16[4,48,512]{2,1,0:T(8,128)(2,1)S(1)}, bf16[4,48,512]{2,1,0:T(8,128)(2,1)S(1)}, u32[]{:S(2)}, u32[]{:S(2)}) collective-permute-start(bf16[4,48,512]{2,1,0:T(8,128)(2,1)S(1)} %pad_maximum_fusion.2.refs_0_), channel_id=1, source_target_pairs={{0,6},{1,7},{2,4},{3,5},{4,2},{5,3},{6,0},{7,1},{8,14},{9,15},{10,... | collective-permute-start | bytes 589832 | tf_op jit(solution)/shard_map/ppermute | solution.py:32
  21.8 7.0 %collective-permute-start.9 = (bf16[144,512]{1,0:T(8,128)(2,1)S(1)}, bf16[144,512]{1,0:T(8,128)(2,1)S(1)}, u32[]{:S(2)}, u32[]{:S(2)}) collective-permute-start(bf16[144,512]{1,0:T(8,128)(2,1)S(1)} %pad_maximum_fusion.9), channel_id=1, source_target_pairs={{0,24},{1,25},{2,26},{3,27},{4,28},{5,29},{6,30},{7,31},{8,16},{9,... | collective-permute-start | bytes 442376 | tf_op jit(solution)/shard_map/ppermute | solution.py:32
  21.9 6.9 %collective-permute-start.7 = (bf16[4,48,512]{2,1,0:T(8,128)(2,1)S(1)}, bf16[4,48,512]{2,1,0:T(8,128)(2,1)S(1)}, u32[]{:S(2)}, u32[]{:S(2)}) collective-permute-start(bf16[4,48,512]{2,1,0:T(8,128)(2,1)S(1)} %pad_maximum_fusion.2.refs_0_), channel_id=1, source_target_pairs={{0,1},{1,0},{2,3},{3,2},{4,5},{5,4},{6,7},{7,6},{8,9},{9,8},{10,11... | collective-permute-start | bytes 589832 | tf_op jit(solution)/shard_map/ppermute | solution.py:32
  22.9 9.0 %collective-permute-start.10 = (bf16[4,48,512]{2,1,0:T(8,128)(2,1)S(1)}, bf16[4,48,512]{2,1,0:T(8,128)(2,1)S(1)}, u32[]{:S(2)}, u32[]{:S(2)}) collective-permute-start(bf16[4,48,512]{2,1,0:T(8,128)(2,1)S(1)} %collective-permute-done.4.refs_1_), channel_id=1, source_target_pairs={{0,1},{1,0},{2,3},{3,2},{4,5},{5,4},{6,7},{7,6},{8,9},{9,8},{10,11... | collective-permute-start | bytes 589832 | tf_op jit(solution)/shard_map/ppermute | solution.py:32
  26.3 6.2 %collective-permute-start.11 = (bf16[4,48,512]{2,1,0:T(8,128)(2,1)S(1)}, bf16[4,48,512]{2,1,0:T(8,128)(2,1)}, u32[]{:S(2)}, u32[]{:S(2)}) collective-permute-start(bf16[4,48,512]{2,1,0:T(8,128)(2,1)S(1)} %collective-permute-done.5.refs_2_), channel_id=1, source_target_pairs={{0,1},{1,0},{2,3},{3,2},{4,5},{5,4},{6,7},{7,6},{8,9},{9,8},{10,11... | collective-permute-start | bytes 589832 | tf_op jit(solution)/shard_map/ppermute | solution.py:32
  28.9 23.7 %collective-permute-start.13 = (bf16[4,144,512]{2,1,0:T(8,128)(2,1)S(1)}, bf16[4,144,512]{2,1,0:T(8,128)(2,1)S(1)}, u32[]{:S(2)}, u32[]{:S(2)}) collective-permute-start(bf16[4,144,512]{2,1,0:T(8,128)(2,1)S(1)} %pad_maximum_fusion.refs_0_), channel_id=1, source_target_pairs={{0,2},{1,3},{2,0},{3,1},{4,6},{5,7},{6,4},{7,5},{8,10},{9,11},{10,... | collective-permute-start | bytes 1769480 | tf_op jit(solution)/shard_map/ppermute | solution.py:32
  30.4 22.2 %collective-permute-start.14 = (bf16[4,144,512]{2,1,0:T(8,128)(2,1)S(1)}, bf16[4,144,512]{2,1,0:T(8,128)(2,1)S(1)}, u32[]{:S(2)}, u32[]{:S(2)}) collective-permute-start(bf16[4,144,512]{2,1,0:T(8,128)(2,1)S(1)} %pad_maximum_fusion.refs_0_), channel_id=1, source_target_pairs={{0,4},{1,5},{2,6},{3,7},{4,0},{5,1},{6,2},{7,3},{8,12},{9,13},{10,... | collective-permute-start | bytes 1769480 | tf_op jit(solution)/shard_map/ppermute | solution.py:32
  31.9 25.2 %collective-permute-start.15 = (bf16[4,144,512]{2,1,0:T(8,128)(2,1)S(1)}, bf16[4,144,512]{2,1,0:T(8,128)(2,1)S(1)}, u32[]{:S(2)}, u32[]{:S(2)}) collective-permute-start(bf16[4,144,512]{2,1,0:T(8,128)(2,1)S(1)} %pad_maximum_fusion.refs_0_), channel_id=1, source_target_pairs={{0,6},{1,7},{2,4},{3,5},{4,2},{5,3},{6,0},{7,1},{8,14},{9,15},{10,... | collective-permute-start | bytes 1769480 | tf_op jit(solution)/shard_map/ppermute | solution.py:32
  32.4 25.9 %collective-permute-start.16 = (bf16[4,144,512]{2,1,0:T(8,128)(2,1)S(1)}, bf16[4,144,512]{2,1,0:T(8,128)(2,1)S(1)}, u32[]{:S(2)}, u32[]{:S(2)}) collective-permute-start(bf16[4,144,512]{2,1,0:T(8,128)(2,1)S(1)} %pad_maximum_fusion.refs_0_), channel_id=1, source_target_pairs={{0,1},{1,0},{2,3},{3,2},{4,5},{5,4},{6,7},{7,6},{8,9},{9,8},{10,11... | collective-permute-start | bytes 1769480 | tf_op jit(solution)/shard_map/ppermute | solution.py:32
  119.9 43.0 %collective-permute-start.22 = (bf16[4,160,512]{2,1,0:T(8,128)(2,1)}, bf16[4,160,512]{2,1,0:T(8,128)(2,1)S(1)}, u32[]{:S(2)}, u32[]{:S(2)}) collective-permute-start(bf16[4,160,512]{2,1,0:T(8,128)(2,1)} %get-tuple-element.138), channel_id=1, source_target_pairs={{0,2},{1,3},{2,0},{3,1},{4,6},{5,7},{6,4},{7,5},{8,10},{9,11},{10,... | collective-permute-start | bytes 1966088 | tf_op jit(solution)/shard_map/ppermute | solution.py:32
  121.1 41.8 %collective-permute-start.23 = (bf16[4,160,512]{2,1,0:T(8,128)(2,1)}, bf16[4,160,512]{2,1,0:T(8,128)(2,1)S(1)}, u32[]{:S(2)}, u32[]{:S(2)}) collective-permute-start(bf16[4,160,512]{2,1,0:T(8,128)(2,1)} %get-tuple-element.139), channel_id=1, source_target_pairs={{0,4},{1,5},{2,6},{3,7},{4,0},{5,1},{6,2},{7,3},{8,12},{9,13},{10,... | collective-permute-start | bytes 1966088 | tf_op jit(solution)/shard_map/ppermute | solution.py:32
  122.3 40.6 %collective-permute-start.24 = (bf16[4,160,512]{2,1,0:T(8,128)(2,1)S(1)}, bf16[4,160,512]{2,1,0:T(8,128)(2,1)}, u32[]{:S(2)}, u32[]{:S(2)}) collective-permute-start(bf16[4,160,512]{2,1,0:T(8,128)(2,1)S(1)} %get-tuple-element.140), channel_id=1, source_target_pairs={{0,6},{1,7},{2,4},{3,5},{4,2},{5,3},{6,0},{7,1},{8,14},{9,15},{10,... | collective-permute-start | bytes 1966088 | tf_op jit(solution)/shard_map/ppermute | solution.py:32
  158.8 6.9 %collective-permute-start.21 = (bf16[16,48,512]{2,1,0:T(8,128)(2,1)}, bf16[16,48,512]{2,1,0:T(8,128)(2,1)S(1)}, u32[]{:S(2)}, u32[]{:S(2)}) collective-permute-start(bf16[16,48,512]{2,1,0:T(8,128)(2,1)} %get-tuple-element.133), channel_id=1, source_target_pairs={{0,1},{1,0},{2,3},{3,2},{4,5},{5,4},{6,7},{7,6},{8,9},{9,8},{10,11... | collective-permute-start | bytes 2359304 | tf_op jit(solution)/shard_map/ppermute | solution.py:32
  166.0 7.6 %collective-permute-start.25 = (bf16[4,48,512]{2,1,0:T(8,128)(2,1)S(1)}, bf16[4,48,512]{2,1,0:T(8,128)(2,1)S(1)}, u32[]{:S(2)}, u32[]{:S(2)}) collective-permute-start(bf16[4,48,512]{2,1,0:T(8,128)(2,1)S(1)} %get-tuple-element.145), channel_id=1, source_target_pairs={{0,4},{1,5},{2,6},{3,7},{4,0},{5,1},{6,2},{7,3},{8,12},{9,13},{10,... | collective-permute-start | bytes 589832 | tf_op jit(solution)/shard_map/ppermute | solution.py:32
  169.7 21.0 %collective-permute-start.26 = (bf16[4,48,512]{2,1,0:T(8,128)(2,1)S(1)}, bf16[4,48,512]{2,1,0:T(8,128)(2,1)S(1)}, u32[]{:S(2)}, u32[]{:S(2)}) collective-permute-start(bf16[4,48,512]{2,1,0:T(8,128)(2,1)S(1)} %get-tuple-element.152), channel_id=1, source_target_pairs={{0,2},{1,3},{2,0},{3,1},{4,6},{5,7},{6,4},{7,5},{8,10},{9,11},{10,... | collective-permute-start | bytes 589832 | tf_op jit(solution)/shard_map/ppermute | solution.py:32
  171.4 19.4 %collective-permute-start.27 = (bf16[4,48,512]{2,1,0:T(8,128)(2,1)S(1)}, bf16[4,48,512]{2,1,0:T(8,128)(2,1)S(1)}, u32[]{:S(2)}, u32[]{:S(2)}) collective-permute-start(bf16[4,48,512]{2,1,0:T(8,128)(2,1)S(1)} %get-tuple-element.153), channel_id=1, source_target_pairs={{0,6},{1,7},{2,4},{3,5},{4,2},{5,3},{6,0},{7,1},{8,14},{9,15},{10,... | collective-permute-start | bytes 589832 | tf_op jit(solution)/shard_map/ppermute | solution.py:32
  172.5 18.2 %collective-permute-start.28 = (bf16[1,160,512]{2,1,0:T(8,128)(2,1)S(1)}, bf16[1,160,512]{2,1,0:T(8,128)(2,1)S(1)}, u32[]{:S(2)}, u32[]{:S(2)}) collective-permute-start(bf16[1,160,512]{2,1,0:T(8,128)(2,1)S(1)} %get-tuple-element.154), channel_id=1, source_target_pairs={{0,8},{1,9},{2,10},{3,11},{4,12},{5,13},{6,14},{7,15},{8,0},{9,1},... | collective-permute-start | bytes 491528 | tf_op jit(solution)/shard_map/ppermute | solution.py:32
  172.8 17.9 %collective-permute-start.29 = (bf16[1,160,512]{2,1,0:T(8,128)(2,1)S(1)}, bf16[1,160,512]{2,1,0:T(8,128)(2,1)S(1)}, u32[]{:S(2)}, u32[]{:S(2)}) collective-permute-start(bf16[1,160,512]{2,1,0:T(8,128)(2,1)S(1)} %get-tuple-element.155), channel_id=1, source_target_pairs={{0,16},{1,17},{2,18},{3,19},{4,20},{5,21},{6,22},{7,23},{8,24},{9,... | collective-permute-start | bytes 491528 | tf_op jit(solution)/shard_map/ppermute | solution.py:32
  173.6 17.1 %collective-permute-start.30 = (bf16[1,160,512]{2,1,0:T(8,128)(2,1)S(1)}, bf16[1,160,512]{2,1,0:T(8,128)(2,1)S(1)}, u32[]{:S(2)}, u32[]{:S(2)}) collective-permute-start(bf16[1,160,512]{2,1,0:T(8,128)(2,1)S(1)} %get-tuple-element.156), channel_id=1, source_target_pairs={{0,24},{1,25},{2,26},{3,27},{4,28},{5,29},{6,30},{7,31},{8,16},{9,... | collective-permute-start | bytes 491528 | tf_op jit(solution)/shard_map/ppermute | solution.py:32
  200.0 8.8 %collective-permute-start.35 = (bf16[112,512]{1,0:T(8,128)(2,1)S(1)}, bf16[112,512]{1,0:T(8,128)(2,1)S(1)}, u32[]{:S(2)}, u32[]{:S(2)}) collective-permute-start(bf16[112,512]{1,0:T(8,128)(2,1)S(1)} %get-tuple-element.275), channel_id=1, source_target_pairs={{0,16},{1,17},{2,18},{3,19},{4,20},{5,21},{6,22},{7,23},{8,24},{9,... | collective-permute-start | bytes 344072 | tf_op jit(solution)/shard_map/ppermute | solution.py:32
  204.0 6.7 %collective-permute-start.36 = (bf16[112,512]{1,0:T(8,128)(2,1)S(1)}, bf16[112,512]{1,0:T(8,128)(2,1)S(1)}, u32[]{:S(2)}, u32[]{:S(2)}) collective-permute-start(bf16[112,512]{1,0:T(8,128)(2,1)S(1)} %get-tuple-element.274), channel_id=1, source_target_pairs={{0,24},{1,25},{2,26},{3,27},{4,28},{5,29},{6,30},{7,31},{8,16},{9,... | collective-permute-start | bytes 344072 | tf_op jit(solution)/shard_map/ppermute | solution.py:32
  211.4 7.0 %collective-permute-start.37 = (bf16[304,512]{1,0:T(8,128)(2,1)S(1)}, bf16[304,512]{1,0:T(8,128)(2,1)S(1)}, u32[]{:S(2)}, u32[]{:S(2)}) collective-permute-start(bf16[304,512]{1,0:T(8,128)(2,1)S(1)} %constant_dynamic-update-slice_fusion.1), channel_id=1, source_target_pairs={{0,4},{1,5},{2,6},{3,7},{4,0},{5,1},{6,2},{7,3},{8,12},{9,13},{10,... | collective-permute-start | bytes 933896 | tf_op jit(solution)/shard_map/ppermute | solution.py:32
  219.2 9.9 %collective-permute-start.38 = (bf16[560,512]{1,0:T(8,128)(2,1)S(1)}, bf16[560,512]{1,0:T(8,128)(2,1)S(1)}, u32[]{:S(2)}, u32[]{:S(2)}) collective-permute-start(bf16[560,512]{1,0:T(8,128)(2,1)S(1)} %get-tuple-element.231), channel_id=1, source_target_pairs={{0,2},{1,3},{2,0},{3,1},{4,6},{5,7},{6,4},{7,5},{8,10},{9,11},{10,... | collective-permute-start | bytes 1720328 | tf_op jit(solution)/shard_map/ppermute | solution.py:32
  253.9 6.8 %collective-permute-start.40 = (bf16[4,16,512]{2,1,0:T(8,128)(2,1)S(1)}, bf16[4,16,512]{2,1,0:T(8,128)(2,1)S(1)}, u32[]{:S(2)}, u32[]{:S(2)}) collective-permute-start(bf16[4,16,512]{2,1,0:T(8,128)(2,1)S(1)} %get-tuple-element.246), channel_id=1, source_target_pairs={{0,8},{1,9},{2,10},{3,11},{4,12},{5,13},{6,14},{7,15},{8,0},{9,1},... | collective-permute-start | bytes 196616 | tf_op jit(solution)/shard_map/ppermute | solution.py:32
  257.4 6.4 %collective-permute-start.42 = (bf16[4,16,512]{2,1,0:T(8,128)(2,1)S(1)}, bf16[4,16,512]{2,1,0:T(8,128)(2,1)S(1)}, u32[]{:S(2)}, u32[]{:S(2)}) collective-permute-start(bf16[4,16,512]{2,1,0:T(8,128)(2,1)S(1)} %get-tuple-element.247), channel_id=1, source_target_pairs={{0,24},{1,25},{2,26},{3,27},{4,28},{5,29},{6,30},{7,31},{8,16},{9,... | collective-permute-start | bytes 196616 | tf_op jit(solution)/shard_map/ppermute | solution.py:32
  (48 other events, 515.5 us)
where the time goes:
time: 267 us; the launch traced here: 266 us
  Pallas kernels  139 us (52%)
  starting transfers between devices  45.8 us (17%)
  waiting for transfers between devices  43.9 us (16%)
  local copies, waits for them, and re-layouts  23.4 us (9%)
  other arithmetic  7.57 us (3%)
  matrix products  3.85 us (1%)
  between operations  2.97 us (1%)
    pallas_call x1, Pallas kernels, feed_forward(): pl.pallas_call(partial(feed_kernel, slots=slots, shard=shard if aligned(s...  47.8 us
    ppermute x43, starting transfers between devices, exchange(): return lax.ppermute(payload, 'dp', [(i, i ^ mask) for i in range(devices)])  45.8 us
    ppermute x43, waiting for transfers between devices, exchange(): return lax.ppermute(payload, 'dp', [(i, i ^ mask) for i in range(devices)])  43.9 us
    pallas_call x1, Pallas kernels, attend_backward(): pl.pallas_call(partial(attend_back_kernel, shard=shard if aligned(shard)...  35.4 us
    pallas_call x1, Pallas kernels, attend_forward(): pl.pallas_call(partial(attend_kernel, pieces=len(sources), shard=shard),...  19.9 us
    pallas_call x1, Pallas kernels, newton_rows(): pl.pallas_call(newton_kernel, out_shape=jax.ShapeDtypeStruct((blocks, chu...  17.4 us
    pallas_call x1, Pallas kernels, input_backward(): pl.pallas_call(input_kernel, grid=(slots // 2,), in_specs=[whole((rows, w...  13.8 us
    unnamed x90, local copies, waits for them, and re-layouts  10.3 us
  transfers between devices with their start and end apart: 43, of which 17 were waited for; matrix products, arithmetic and copies ran while one was open for 7% of the time, Pallas kernels for 27%

commit v1 on v0

--- a/solution.py
+++ b/solution.py
@@ -295,7 +295,9 @@
         return high, (values - high.astype(jnp.float32)).astype(jnp.bfloat16)
 
     def product(left, right):
-        return dot(left[0], right[0]) + (dot(left[1], right[0]) + dot(left[0], right[1]))
+        return dot(
+            jnp.concatenate([left[0], left[1], left[0]], axis=1), jnp.concatenate([right[0], right[0], right[1]], axis=0)
+        )
 
     def mix(gram, parts):
         return halves(newton_first * eye + newton_second * gram + newton_third * product(parts, parts))
@@ -371,15 +373,31 @@
         got = exchange(jnp.concatenate([give, sent]), devices, CELL * step)
         pieces.append(got[:rows])
         sums.append(value(got[rows:]))
-    current = jnp.concatenate(pieces)
+    half = rows // 2
+    left = jnp.concatenate([piece[:half] for piece in pieces])
+    right = jnp.concatenate([piece[half:] for piece in pieces])
+    length = left.shape[0]
     total = add_tree(sums)
-    for mask in (4, 2, 1):
-        sent = pair(total)
-        got = exchange(jnp.concatenate([current, sent]), devices, mask)
-        length = current.shape[0]
-        current = jnp.concatenate([current, got[:length]])
-        total = value(sent) + value(got[length:])
-    return current.reshape(CELL, planes, rows, LANE), total
+    sent = pair(total)
+    got = exchange(jnp.concatenate([left, sent]), devices, 4)
+    got, right_x = lax.optimization_barrier((got, exchange(right, devices, 2)))
+    total = value(sent) + value(got[length:])
+    left = jnp.concatenate([left, got[:length]])
+    sent = pair(total)
+    got = exchange(jnp.concatenate([left, sent]), devices, 2)
+    got, right_y = lax.optimization_barrier((got, exchange(jnp.concatenate([right, right_x]), devices, 4)))
+    total = value(sent) + value(got[2 * length :])
+    left = jnp.concatenate([left, got[: 2 * length]])
+    right = jnp.concatenate([right, right_y[:length], right_x, right_y[length:]])
+    sent = pair(total)
+    current = jnp.concatenate([left, right])
+    got = exchange(jnp.concatenate([current, sent]), devices, 1)
+    total = value(sent) + value(got[2 * 4 * length :])
+    halves = jnp.concatenate(
+        [values.reshape(2, 4 * planes, half, LANE) for values in (current, got[: 8 * length])], axis=1
+    )
+    current = jnp.swapaxes(halves, 0, 1).reshape(CELL, planes, rows, LANE)
+    return current, total
 
 
 PAD_TOK = 64
@@ -959,9 +977,12 @@
         (input_sums, head_got[0], head_got[2], *body_got)
     )
     input_grad = image_form(input_rows, slots)
-    table_term = table_gradient(table_sums, one_hot)
     head_own, head_sends = fold(head_own[None], [got[None] for got in head_got], plane, HEAD, shard)
     head_got = send_all(head_sends, CELL, devices)
+    head_got[0], table_sums, triple_sums, hidden_sums = lax.optimization_barrier(
+        (head_got[0], table_sums, triple_sums, hidden_sums)
+    )
+    table_term = table_gradient(table_sums, one_hot)
     momenta = (attend_momentum, merge_momentum, expand_momentum, project_momentum)
     grads, following, packed = finish(head_own, head_got, body_own, body_got, momenta, shard, grad_scale)
 

time: 267 us -> 255 us (0.955)
  local copies, waits for them, and re-layouts: 23.4 us -> 15.1 us
    unnamed x90 -> x102, local copies, waits for them, and re-layouts: 10.3 us -> 6.18 us
    ppermute x43 -> x45, waiting for transfers between devices: 43.9 us -> 42.1 us  [exchange(): return lax.ppermute(payload, 'dp', [(i, i ^ mask) for i in range(devices)])]
    ppermute x43 -> x45, starting transfers between devices: 45.8 us -> 45.7 us  [exchange(): return lax.ppermute(payload, 'dp', [(i, i ^ mask) for i in range(devices)])]
  transfers between devices with their start and end apart: 43 -> 45, of which waited for: 17 -> 15; matrix products, arithmetic and copies ran while one was open for 7% -> 5% of each run, Pallas kernels for 27% -> 28%
where the time goes in v1:
time: 255 us; the launch traced here: 254 us
  Pallas kernels  138 us (54%)
  starting transfers between devices  45.7 us (18%)
  waiting for transfers between devices  42.1 us (17%)
  local copies, waits for them, and re-layouts  15.1 us (6%)
  other arithmetic  6.58 us (3%)
  between operations  3.19 us (1%)
  matrix products  3.14 us (1%)
    pallas_call x1, Pallas kernels, feed_forward(): pl.pallas_call(partial(feed_kernel, slots=slots, shard=shard if aligned(s...  47.8 us
    ppermute x45, starting transfers between devices, exchange(): return lax.ppermute(payload, 'dp', [(i, i ^ mask) for i in range(devices)])  45.7 us
    ppermute x45, waiting for transfers between devices, exchange(): return lax.ppermute(payload, 'dp', [(i, i ^ mask) for i in range(devices)])  42.1 us
    pallas_call x1, Pallas kernels, attend_backward(): pl.pallas_call(partial(attend_back_kernel, shard=shard if aligned(shard)...  35.2 us
    pallas_call x1, Pallas kernels, attend_forward(): pl.pallas_call(partial(attend_kernel, pieces=len(sources), shard=shard),...  20 us
    pallas_call x1, Pallas kernels, newton_rows(): pl.pallas_call(newton_kernel, out_shape=jax.ShapeDtypeStruct((blocks, chu...  17.1 us
    pallas_call x1, Pallas kernels, input_backward(): pl.pallas_call(input_kernel, grid=(slots // 2,), in_specs=[whole((rows, w...  13.8 us
    unnamed x102, local copies, waits for them, and re-layouts  6.18 us
  transfers between devices with their start and end apart: 45, of which 15 were waited for; matrix products, arithmetic and copies ran while one was open for 5% of the time, Pallas kernels for 28%

profile of v1, /device:TPU:0, one launch (start us, length us, event | category | flops | bytes accessed | tf_op | source)
XLA Modules:
  0.0 254.3 jit_solution(12729888215757562305)
XLA Ops:
  1.5 3.1 %collective-permute-start = (bf16[48,512]{1,0:T(8,128)(2,1)S(1)}, bf16[48,512]{1,0:T(8,128)(2,1)S(1)}, u32[]{:S(2)}, u32[]{:S(2)}) collective-permute-start(bf16[48,512]{1,0:T(8,128)(2,1)S(1)} %bitcast.154), channel_id=1, source_target_pairs={{0,8},{1,9},{2,10},{3,11},{4,12},{5,13},{6,14},{7,15},{8,0},{9,1},... | collective-permute-start | bytes 147464 | tf_op jit(solution)/shard_map/ppermute | solution.py:32
  4.6 2.6 %collective-permute-start.1 = (bf16[48,512]{1,0:T(8,128)(2,1)S(1)}, bf16[48,512]{1,0:T(8,128)(2,1)S(1)}, u32[]{:S(2)}, u32[]{:S(2)}) collective-permute-start(bf16[48,512]{1,0:T(8,128)(2,1)S(1)} %bitcast.155), channel_id=1, source_target_pairs={{0,16},{1,17},{2,18},{3,19},{4,20},{5,21},{6,22},{7,23},{8,24},{9,... | collective-permute-start | bytes 147464 | tf_op jit(solution)/shard_map/ppermute | solution.py:32
  9.9 3.5 %collective-permute-start.8 = (bf16[144,512]{1,0:T(8,128)(2,1)S(1)}, bf16[144,512]{1,0:T(8,128)(2,1)S(1)}, u32[]{:S(2)}, u32[]{:S(2)}) collective-permute-start(bf16[144,512]{1,0:T(8,128)(2,1)S(1)} %pad_maximum_fusion.10), channel_id=1, source_target_pairs={{0,16},{1,17},{2,18},{3,19},{4,20},{5,21},{6,22},{7,23},{8,24},{9,... | collective-permute-start | bytes 442376 | tf_op jit(solution)/shard_map/ppermute | solution.py:32
  15.3 1.6 collective-permute-start.4
  16.8 1.5 collective-permute-start.5
  21.2 1.7 collective-permute-done.4.refs_1_
  23.0 3.3 %collective-permute-done.5.refs_2_ = bf16[4,48,512]{2,1,0:T(8,128)(2,1)S(1)} collective-permute-done((bf16[4,48,512]{2,1,0:T(8,128)(2,1)S(1)}, bf16[4,48,512]{2,1,0:T(8,128)(2,1)S(1)}, u32[]{:S(2)}, u32[]{:S(2)}) %collective-permute-start.5) | collective-permute-done | bytes 196640 | tf_op jit(solution)/shard_map/ppermute | solution.py:32
  32.2 20.0 %attend_forward.1 = (bf16[8,256,512]{2,1,0:T(8,128)(2,1)}, bf16[8,256,1536]{2,1,0:T(8,128)(2,1)}, bf16[8,4,4,64,256]{4,3,2,1,0:T(8,128)(2,1)}, f32[4,1568,128]{2,1,0:T(8,128)}, bf16[3,512,512]{2,1,0:T(8,128)(2,1)}) custom-call(s32[1]{0:T(128)} %bitcast.rank_ref, bf16[1568,512]{1,0:T(8,128)(2,1)} %bitcast.177, f32[2,512]{1,0:T(2,128)} %gains_ref.5, ...), custom_call_target="tpu_custom_call" | custom-call | flops 20000000000 | bytes 16777216 | tf_op jit(solution)/shard_map/attend_forward/pallas_call | solution.py:543
  52.2 5.1 %collective-permute-done.15.refs_3_ = bf16[4,144,512]{2,1,0:T(8,128)(2,1)S(1)} collective-permute-done((bf16[4,144,512]{2,1,0:T(8,128)(2,1)S(1)}, bf16[4,144,512]{2,1,0:T(8,128)(2,1)S(1)}, u32[]{:S(2)}, u32[]{:S(2)}) %collective-permute-start.15) | collective-permute-done | bytes 589856 | tf_op jit(solution)/shard_map/ppermute | solution.py:32
  61.8 47.8 %feed_forward.1 = (bf16[1568,512]{1,0:T(8,128)(2,1)}, f32[4,1568,128]{2,1,0:T(8,128)}, f32[4,1568,128]{2,1,0:T(8,128)}, f32[8,512]{1,0:T(8,128)}, f32[8,2048]{1,...) custom-call(s32[1]{0:T(128)S(6)} %copy.170.count_ref, s32[1]{0:T(128)} %bitcast.rank_ref, ...), custom_call_target="tpu_custom_call" | custom-call | flops 44000002048 | bytes 16777216 | tf_op jit(solution)/shard_map/feed_forward/pallas_call | solution.py:664
  109.9 5.0 %collective-permute-done.20 = bf16[16,160,512]{2,1,0:T(8,128)(2,1)S(1)} collective-permute-done((bf16[16,160,512]{2,1,0:T(8,128)(2,1)}, bf16[16,160,512]{2,1,0:T(8,128)(2,1)S(1)}, u32[]{:S(2)}, u32[]{:S(2)}) %collective-permute-start.20) | collective-permute-done | bytes 2621472 | tf_op jit(solution)/shard_map/ppermute | solution.py:32
  114.8 2.3 copy-done.4
  117.2 1.8 fold.4
  123.5 35.2 %attend_backward.1 = (bf16[8,256,1536]{2,1,0:T(8,128)(2,1)}, f32[4,56,256]{2,1,0:T(8,128)}, f32[8,1536]{1,0:T(8,128)}, f32[16,48,512]{2,1,0:T(8,128)}, bf16[16,48,512]{2,1,0:T(8,128)(2,1)}) custom-call(s32[1]{0:T(128)} %bitcast.24.mine_ref, f32[4,1568,128]{2,1,0:T(8,128)} %get-tuple-element.135.grad_mixed_ref, ...), custom_call_target="tpu_custom_call" | custom-call | flops 36999999488 | bytes 16777216 | tf_op jit(solution)/shard_map/attend_backward/pallas_call | solution.py:754
  160.1 1.5 fold.6
  162.8 1.6 collective-permute-start.26
  166.4 2.8 %collective-permute-done.25 = bf16[4,48,512]{2,1,0:T(8,128)(2,1)S(1)} collective-permute-done((bf16[4,48,512]{2,1,0:T(8,128)(2,1)S(1)}, bf16[4,48,512]{2,1,0:T(8,128)(2,1)S(1)}, u32[]{:S(2)}, u32[]{:S(2)}) %collective-permute-start.25) | collective-permute-done | bytes 196640 | tf_op jit(solution)/shard_map/ppermute | solution.py:32
  170.0 13.8 %input_backward.1 = (f32[1568,512]{1,0:T(8,128)}, f32[8,512]{1,0:T(8,128)}) custom-call(bf16[1568,512]{1,0:T(8,128)(2,1)} %bitcast.179, bf16[8,256,1536]{2,1,0:T(8,128)(2,1)} %get-tuple-element.154.grad_triple_ref, f32[4,1568,128]{2,1,0:T(8,128)} %get-tuple-element.155.grad_middle_ref, bf16[3,512,512]{2,1,0:T(8,128)(2,1)} %get-tuple-element.156.weights_ref, ...), custom_call_target="tpu_custom_call" | custom-call | flops 14000000000 | bytes 16777216 | tf_op jit(solution)/shard_map/input_backward/pallas_call | solution.py:808
  185.0 3.5 %collective-permute-start.32 = (bf16[1,48,512]{2,1,0:T(8,128)(2,1)S(1)}, bf16[1,48,512]{2,1,0:T(8,128)(2,1)S(1)}, u32[]{:S(2)}, u32[]{:S(2)}) collective-permute-start(bf16[1,48,512]{2,1,0:T(8,128)(2,1)S(1)} %get-tuple-element.175), channel_id=1, source_target_pairs={{0,16},{1,17},{2,18},{3,19},{4,20},{5,21},{6,22},{7,23},{8,24},{9,... | collective-permute-start | bytes 147464 | tf_op jit(solution)/shard_map/ppermute | solution.py:32
  191.4 1.9 fusion.1
  195.5 2.8 %collective-permute-start.35 = (bf16[112,512]{1,0:T(8,128)(2,1)S(1)}, bf16[112,512]{1,0:T(8,128)(2,1)S(1)}, u32[]{:S(2)}, u32[]{:S(2)}) collective-permute-start(bf16[112,512]{1,0:T(8,128)(2,1)S(1)} %get-tuple-element.309), channel_id=1, source_target_pairs={{0,16},{1,17},{2,18},{3,19},{4,20},{5,21},{6,22},{7,23},{8,24},{9,... | collective-permute-start | bytes 344072 | tf_op jit(solution)/shard_map/ppermute | solution.py:32
  198.3 1.6 collective-permute-start.36
  200.9 5.0 %collective-permute-done.35 = bf16[112,512]{1,0:T(8,128)(2,1)S(1)} collective-permute-done((bf16[112,512]{1,0:T(8,128)(2,1)S(1)}, bf16[112,512]{1,0:T(8,128)(2,1)S(1)}, u32[]{:S(2)}, u32[]{:S(2)}) %collective-permute-start.35) | collective-permute-done | bytes 114720 | tf_op jit(solution)/shard_map/ppermute | solution.py:32
  207.0 1.6 collective-permute-start.38
  208.6 4.8 %collective-permute-done.38 = bf16[128,512]{1,0:T(8,128)(2,1)S(1)} collective-permute-done((bf16[128,512]{1,0:T(8,128)(2,1)S(1)}, bf16[128,512]{1,0:T(8,128)(2,1)S(1)}, u32[]{:S(2)}, u32[]{:S(2)}) %collective-permute-start.38) | collective-permute-done | bytes 131104 | tf_op jit(solution)/shard_map/ppermute | solution.py:32
  213.4 1.6 collective-permute-start.39
  215.9 5.6 %collective-permute-done.40 = bf16[256,512]{1,0:T(8,128)(2,1)S(1)} collective-permute-done((bf16[256,512]{1,0:T(8,128)(2,1)S(1)}, bf16[256,512]{1,0:T(8,128)(2,1)S(1)}, u32[]{:S(2)}, u32[]{:S(2)}) %collective-permute-start.40) | collective-permute-done | bytes 262176 | tf_op jit(solution)/shard_map/ppermute | solution.py:32
  222.6 2.0 collective-permute-done.41
  225.6 17.1 %newton_rows.1 = bf16[4,64,512]{2,1,0:T(8,128)(2,1)S(1)} custom-call(s32[1]{0:T(128)} %bitcast.41.kind_ref, bf16[4,512,512]{2,1,0:T(8,128)(2,1)S(1)} %bitcast.132), custom_call_target="tpu_custom_call" | custom-call | flops 20000000000 | bytes 4194304 | tf_op jit(solution)/shard_map/newton_rows/pallas_call | solution.py:335
  243.3 1.7 collective-permute-start.43
  245.1 2.2 collective-permute-start.44
  249.2 2.4 collective-permute-done.43
  (233 shorter events, 43.1 us)
Async XLA Ops:
  1.5 13.6 %collective-permute-start = (bf16[48,512]{1,0:T(8,128)(2,1)S(1)}, bf16[48,512]{1,0:T(8,128)(2,1)S(1)}, u32[]{:S(2)}, u32[]{:S(2)}) collective-permute-start(bf16[48,512]{1,0:T(8,128)(2,1)S(1)} %bitcast.154), channel_id=1, source_target_pairs={{0,8},{1,9},{2,10},{3,11},{4,12},{5,13},{6,14},{7,15},{8,0},{9,1},... | collective-permute-start | bytes 147464 | tf_op jit(solution)/shard_map/ppermute | solution.py:32
  4.6 10.5 %collective-permute-start.1 = (bf16[48,512]{1,0:T(8,128)(2,1)S(1)}, bf16[48,512]{1,0:T(8,128)(2,1)S(1)}, u32[]{:S(2)}, u32[]{:S(2)}) collective-permute-start(bf16[48,512]{1,0:T(8,128)(2,1)S(1)} %bitcast.155), channel_id=1, source_target_pairs={{0,16},{1,17},{2,18},{3,19},{4,20},{5,21},{6,22},{7,23},{8,24},{9,... | collective-permute-start | bytes 147464 | tf_op jit(solution)/shard_map/ppermute | solution.py:32
  7.2 8.0 %collective-permute-start.2 = (bf16[48,512]{1,0:T(8,128)(2,1)S(1)}, bf16[48,512]{1,0:T(8,128)(2,1)S(1)}, u32[]{:S(2)}, u32[]{:S(2)}) collective-permute-start(bf16[48,512]{1,0:T(8,128)(2,1)S(1)} %bitcast.156), channel_id=1, source_target_pairs={{0,24},{1,25},{2,26},{3,27},{4,28},{5,29},{6,30},{7,31},{8,16},{9,... | collective-permute-start | bytes 147464 | tf_op jit(solution)/shard_map/ppermute | solution.py:32
  8.9 12.1 %collective-permute-start.3 = (bf16[144,512]{1,0:T(8,128)(2,1)S(1)}, bf16[144,512]{1,0:T(8,128)(2,1)S(1)}, u32[]{:S(2)}, u32[]{:S(2)}) collective-permute-start(bf16[144,512]{1,0:T(8,128)(2,1)S(1)} %pad_maximum_fusion.10), channel_id=1, source_target_pairs={{0,8},{1,9},{2,10},{3,11},{4,12},{5,13},{6,14},{7,15},{8,0},{9,1},... | collective-permute-start | bytes 442376 | tf_op jit(solution)/shard_map/ppermute | solution.py:32
  9.9 11.3 %collective-permute-start.8 = (bf16[144,512]{1,0:T(8,128)(2,1)S(1)}, bf16[144,512]{1,0:T(8,128)(2,1)S(1)}, u32[]{:S(2)}, u32[]{:S(2)}) collective-permute-start(bf16[144,512]{1,0:T(8,128)(2,1)S(1)} %pad_maximum_fusion.10), channel_id=1, source_target_pairs={{0,16},{1,17},{2,18},{3,19},{4,20},{5,21},{6,22},{7,23},{8,24},{9,... | collective-permute-start | bytes 442376 | tf_op jit(solution)/shard_map/ppermute | solution.py:32
  15.3 7.7 %collective-permute-start.4 = (bf16[4,48,512]{2,1,0:T(8,128)(2,1)S(1)}, bf16[4,48,512]{2,1,0:T(8,128)(2,1)S(1)}, u32[]{:S(2)}, u32[]{:S(2)}) collective-permute-start(bf16[4,48,512]{2,1,0:T(8,128)(2,1)S(1)} %pad_maximum_fusion.3.refs_0_), channel_id=1, source_target_pairs={{0,2},{1,3},{2,0},{3,1},{4,6},{5,7},{6,4},{7,5},{8,10},{9,11},{10,... | collective-permute-start | bytes 589832 | tf_op jit(solution)/shard_map/ppermute | solution.py:32
  16.8 9.5 %collective-permute-start.5 = (bf16[4,48,512]{2,1,0:T(8,128)(2,1)S(1)}, bf16[4,48,512]{2,1,0:T(8,128)(2,1)S(1)}, u32[]{:S(2)}, u32[]{:S(2)}) collective-permute-start(bf16[4,48,512]{2,1,0:T(8,128)(2,1)S(1)} %pad_maximum_fusion.3.refs_0_), channel_id=1, source_target_pairs={{0,4},{1,5},{2,6},{3,7},{4,0},{5,1},{6,2},{7,3},{8,12},{9,13},{10,... | collective-permute-start | bytes 589832 | tf_op jit(solution)/shard_map/ppermute | solution.py:32
  18.3 8.0 %collective-permute-start.6 = (bf16[4,48,512]{2,1,0:T(8,128)(2,1)S(1)}, bf16[4,48,512]{2,1,0:T(8,128)(2,1)S(1)}, u32[]{:S(2)}, u32[]{:S(2)}) collective-permute-start(bf16[4,48,512]{2,1,0:T(8,128)(2,1)S(1)} %pad_maximum_fusion.3.refs_0_), channel_id=1, source_target_pairs={{0,6},{1,7},{2,4},{3,5},{4,2},{5,3},{6,0},{7,1},{8,14},{9,15},{10,... | collective-permute-start | bytes 589832 | tf_op jit(solution)/shard_map/ppermute | solution.py:32
  21.1 7.4 %collective-permute-start.9 = (bf16[144,512]{1,0:T(8,128)(2,1)S(1)}, bf16[144,512]{1,0:T(8,128)(2,1)S(1)}, u32[]{:S(2)}, u32[]{:S(2)}) collective-permute-start(bf16[144,512]{1,0:T(8,128)(2,1)S(1)} %pad_maximum_fusion.10), channel_id=1, source_target_pairs={{0,24},{1,25},{2,26},{3,27},{4,28},{5,29},{6,30},{7,31},{8,16},{9,... | collective-permute-start | bytes 442376 | tf_op jit(solution)/shard_map/ppermute | solution.py:32
  21.2 7.3 %collective-permute-start.7 = (bf16[4,48,512]{2,1,0:T(8,128)(2,1)S(1)}, bf16[4,48,512]{2,1,0:T(8,128)(2,1)S(1)}, u32[]{:S(2)}, u32[]{:S(2)}) collective-permute-start(bf16[4,48,512]{2,1,0:T(8,128)(2,1)S(1)} %pad_maximum_fusion.3.refs_0_), channel_id=1, source_target_pairs={{0,1},{1,0},{2,3},{3,2},{4,5},{5,4},{6,7},{7,6},{8,9},{9,8},{10,11... | collective-permute-start | bytes 589832 | tf_op jit(solution)/shard_map/ppermute | solution.py:32
  23.0 8.3 %collective-permute-start.10 = (bf16[4,48,512]{2,1,0:T(8,128)(2,1)S(1)}, bf16[4,48,512]{2,1,0:T(8,128)(2,1)S(1)}, u32[]{:S(2)}, u32[]{:S(2)}) collective-permute-start(bf16[4,48,512]{2,1,0:T(8,128)(2,1)S(1)} %collective-permute-done.4.refs_1_), channel_id=1, source_target_pairs={{0,1},{1,0},{2,3},{3,2},{4,5},{5,4},{6,7},{7,6},{8,9},{9,8},{10,11... | collective-permute-start | bytes 589832 | tf_op jit(solution)/shard_map/ppermute | solution.py:32
  28.6 23.6 %collective-permute-start.13 = (bf16[4,144,512]{2,1,0:T(8,128)(2,1)S(1)}, bf16[4,144,512]{2,1,0:T(8,128)(2,1)S(1)}, u32[]{:S(2)}, u32[]{:S(2)}) collective-permute-start(bf16[4,144,512]{2,1,0:T(8,128)(2,1)S(1)} %pad_maximum_fusion.1.refs_0_), channel_id=1, source_target_pairs={{0,2},{1,3},{2,0},{3,1},{4,6},{5,7},{6,4},{7,5},{8,10},{9,11},{10,... | collective-permute-start | bytes 1769480 | tf_op jit(solution)/shard_map/ppermute | solution.py:32
  29.8 22.4 %collective-permute-start.14 = (bf16[4,144,512]{2,1,0:T(8,128)(2,1)S(1)}, bf16[4,144,512]{2,1,0:T(8,128)(2,1)S(1)}, u32[]{:S(2)}, u32[]{:S(2)}) collective-permute-start(bf16[4,144,512]{2,1,0:T(8,128)(2,1)S(1)} %pad_maximum_fusion.1.refs_0_), channel_id=1, source_target_pairs={{0,4},{1,5},{2,6},{3,7},{4,0},{5,1},{6,2},{7,3},{8,12},{9,13},{10,... | collective-permute-start | bytes 1769480 | tf_op jit(solution)/shard_map/ppermute | solution.py:32
  31.3 26.0 %collective-permute-start.15 = (bf16[4,144,512]{2,1,0:T(8,128)(2,1)S(1)}, bf16[4,144,512]{2,1,0:T(8,128)(2,1)S(1)}, u32[]{:S(2)}, u32[]{:S(2)}) collective-permute-start(bf16[4,144,512]{2,1,0:T(8,128)(2,1)S(1)} %pad_maximum_fusion.1.refs_0_), channel_id=1, source_target_pairs={{0,6},{1,7},{2,4},{3,5},{4,2},{5,3},{6,0},{7,1},{8,14},{9,15},{10,... | collective-permute-start | bytes 1769480 | tf_op jit(solution)/shard_map/ppermute | solution.py:32
  32.1 26.3 %collective-permute-start.16 = (bf16[4,144,512]{2,1,0:T(8,128)(2,1)S(1)}, bf16[4,144,512]{2,1,0:T(8,128)(2,1)S(1)}, u32[]{:S(2)}, u32[]{:S(2)}) collective-permute-start(bf16[4,144,512]{2,1,0:T(8,128)(2,1)S(1)} %pad_maximum_fusion.1.refs_0_), channel_id=1, source_target_pairs={{0,1},{1,0},{2,3},{3,2},{4,5},{5,4},{6,7},{7,6},{8,9},{9,8},{10,11... | collective-permute-start | bytes 1769480 | tf_op jit(solution)/shard_map/ppermute | solution.py:32
  120.0 38.8 %collective-permute-start.22 = (bf16[4,160,512]{2,1,0:T(8,128)(2,1)}, bf16[4,160,512]{2,1,0:T(8,128)(2,1)S(1)}, u32[]{:S(2)}, u32[]{:S(2)}) collective-permute-start(bf16[4,160,512]{2,1,0:T(8,128)(2,1)} %get-tuple-element.146), channel_id=1, source_target_pairs={{0,2},{1,3},{2,0},{3,1},{4,6},{5,7},{6,4},{7,5},{8,10},{9,11},{10,... | collective-permute-start | bytes 1966088 | tf_op jit(solution)/shard_map/ppermute | solution.py:32
  121.2 37.6 %collective-permute-start.23 = (bf16[4,160,512]{2,1,0:T(8,128)(2,1)}, bf16[4,160,512]{2,1,0:T(8,128)(2,1)S(1)}, u32[]{:S(2)}, u32[]{:S(2)}) collective-permute-start(bf16[4,160,512]{2,1,0:T(8,128)(2,1)} %get-tuple-element.147), channel_id=1, source_target_pairs={{0,4},{1,5},{2,6},{3,7},{4,0},{5,1},{6,2},{7,3},{8,12},{9,13},{10,... | collective-permute-start | bytes 1966088 | tf_op jit(solution)/shard_map/ppermute | solution.py:32
  122.4 36.4 %collective-permute-start.24 = (bf16[4,160,512]{2,1,0:T(8,128)(2,1)S(1)}, bf16[4,160,512]{2,1,0:T(8,128)(2,1)}, u32[]{:S(2)}, u32[]{:S(2)}) collective-permute-start(bf16[4,160,512]{2,1,0:T(8,128)(2,1)S(1)} %get-tuple-element.148), channel_id=1, source_target_pairs={{0,6},{1,7},{2,4},{3,5},{4,2},{5,3},{6,0},{7,1},{8,14},{9,15},{10,... | collective-permute-start | bytes 1966088 | tf_op jit(solution)/shard_map/ppermute | solution.py:32
  161.9 7.3 %collective-permute-start.25 = (bf16[4,48,512]{2,1,0:T(8,128)(2,1)S(1)}, bf16[4,48,512]{2,1,0:T(8,128)(2,1)S(1)}, u32[]{:S(2)}, u32[]{:S(2)}) collective-permute-start(bf16[4,48,512]{2,1,0:T(8,128)(2,1)S(1)} %get-tuple-element.153), channel_id=1, source_target_pairs={{0,4},{1,5},{2,6},{3,7},{4,0},{5,1},{6,2},{7,3},{8,12},{9,13},{10,... | collective-permute-start | bytes 589832 | tf_op jit(solution)/shard_map/ppermute | solution.py:32
  162.8 21.0 %collective-permute-start.26 = (bf16[4,48,512]{2,1,0:T(8,128)(2,1)S(1)}, bf16[4,48,512]{2,1,0:T(8,128)(2,1)S(1)}, u32[]{:S(2)}, u32[]{:S(2)}) collective-permute-start(bf16[4,48,512]{2,1,0:T(8,128)(2,1)S(1)} %get-tuple-element.160), channel_id=1, source_target_pairs={{0,2},{1,3},{2,0},{3,1},{4,6},{5,7},{6,4},{7,5},{8,10},{9,11},{10,... | collective-permute-start | bytes 589832 | tf_op jit(solution)/shard_map/ppermute | solution.py:32
  164.5 19.4 %collective-permute-start.27 = (bf16[4,48,512]{2,1,0:T(8,128)(2,1)S(1)}, bf16[4,48,512]{2,1,0:T(8,128)(2,1)S(1)}, u32[]{:S(2)}, u32[]{:S(2)}) collective-permute-start(bf16[4,48,512]{2,1,0:T(8,128)(2,1)S(1)} %get-tuple-element.161), channel_id=1, source_target_pairs={{0,6},{1,7},{2,4},{3,5},{4,2},{5,3},{6,0},{7,1},{8,14},{9,15},{10,... | collective-permute-start | bytes 589832 | tf_op jit(solution)/shard_map/ppermute | solution.py:32
  165.6 18.2 %collective-permute-start.28 = (bf16[1,160,512]{2,1,0:T(8,128)(2,1)S(1)}, bf16[1,160,512]{2,1,0:T(8,128)(2,1)S(1)}, u32[]{:S(2)}, u32[]{:S(2)}) collective-permute-start(bf16[1,160,512]{2,1,0:T(8,128)(2,1)S(1)} %get-tuple-element.162), channel_id=1, source_target_pairs={{0,8},{1,9},{2,10},{3,11},{4,12},{5,13},{6,14},{7,15},{8,0},{9,1},... | collective-permute-start | bytes 491528 | tf_op jit(solution)/shard_map/ppermute | solution.py:32
  165.9 17.9 %collective-permute-start.29 = (bf16[1,160,512]{2,1,0:T(8,128)(2,1)S(1)}, bf16[1,160,512]{2,1,0:T(8,128)(2,1)S(1)}, u32[]{:S(2)}, u32[]{:S(2)}) collective-permute-start(bf16[1,160,512]{2,1,0:T(8,128)(2,1)S(1)} %get-tuple-element.163), channel_id=1, source_target_pairs={{0,16},{1,17},{2,18},{3,19},{4,20},{5,21},{6,22},{7,23},{8,24},{9,... | collective-permute-start | bytes 491528 | tf_op jit(solution)/shard_map/ppermute | solution.py:32
  169.2 14.6 %collective-permute-start.30 = (bf16[1,160,512]{2,1,0:T(8,128)(2,1)S(1)}, bf16[1,160,512]{2,1,0:T(8,128)(2,1)S(1)}, u32[]{:S(2)}, u32[]{:S(2)}) collective-permute-start(bf16[1,160,512]{2,1,0:T(8,128)(2,1)S(1)} %get-tuple-element.164), channel_id=1, source_target_pairs={{0,24},{1,25},{2,26},{3,27},{4,28},{5,29},{6,30},{7,31},{8,16},{9,... | collective-permute-start | bytes 491528 | tf_op jit(solution)/shard_map/ppermute | solution.py:32
  185.0 8.6 %collective-permute-start.32 = (bf16[1,48,512]{2,1,0:T(8,128)(2,1)S(1)}, bf16[1,48,512]{2,1,0:T(8,128)(2,1)S(1)}, u32[]{:S(2)}, u32[]{:S(2)}) collective-permute-start(bf16[1,48,512]{2,1,0:T(8,128)(2,1)S(1)} %get-tuple-element.175), channel_id=1, source_target_pairs={{0,16},{1,17},{2,18},{3,19},{4,20},{5,21},{6,22},{7,23},{8,24},{9,... | collective-permute-start | bytes 147464 | tf_op jit(solution)/shard_map/ppermute | solution.py:32
  195.5 10.5 %collective-permute-start.35 = (bf16[112,512]{1,0:T(8,128)(2,1)S(1)}, bf16[112,512]{1,0:T(8,128)(2,1)S(1)}, u32[]{:S(2)}, u32[]{:S(2)}) collective-permute-start(bf16[112,512]{1,0:T(8,128)(2,1)S(1)} %get-tuple-element.309), channel_id=1, source_target_pairs={{0,16},{1,17},{2,18},{3,19},{4,20},{5,21},{6,22},{7,23},{8,24},{9,... | collective-permute-start | bytes 344072 | tf_op jit(solution)/shard_map/ppermute | solution.py:32
  198.3 7.7 %collective-permute-start.36 = (bf16[112,512]{1,0:T(8,128)(2,1)S(1)}, bf16[112,512]{1,0:T(8,128)(2,1)S(1)}, u32[]{:S(2)}, u32[]{:S(2)}) collective-permute-start(bf16[112,512]{1,0:T(8,128)(2,1)S(1)} %get-tuple-element.308), channel_id=1, source_target_pairs={{0,24},{1,25},{2,26},{3,27},{4,28},{5,29},{6,30},{7,31},{8,16},{9,... | collective-permute-start | bytes 344072 | tf_op jit(solution)/shard_map/ppermute | solution.py:32
  206.1 7.3 %collective-permute-start.37 = (bf16[176,512]{1,0:T(8,128)(2,1)S(1)}, bf16[176,512]{1,0:T(8,128)(2,1)S(1)}, u32[]{:S(2)}, u32[]{:S(2)}) collective-permute-start(bf16[176,512]{1,0:T(8,128)(2,1)S(1)} %constant_dynamic-update-slice_fusion.1), channel_id=1, source_target_pairs={{0,4},{1,5},{2,6},{3,7},{4,0},{5,1},{6,2},{7,3},{8,12},{9,13},{10,... | collective-permute-start | bytes 540680 | tf_op jit(solution)/shard_map/ppermute | solution.py:32
  213.4 8.1 %collective-permute-start.39 = (bf16[304,512]{1,0:T(8,128)(2,1)S(1)}, bf16[304,512]{1,0:T(8,128)(2,1)S(1)}, u32[]{:S(2)}, u32[]{:S(2)}) collective-permute-start(bf16[304,512]{1,0:T(8,128)(2,1)S(1)} %get-tuple-element.249), channel_id=1, source_target_pairs={{0,2},{1,3},{2,0},{3,1},{4,6},{5,7},{6,4},{7,5},{8,10},{9,11},{10,... | collective-permute-start | bytes 933896 | tf_op jit(solution)/shard_map/ppermute | solution.py:32
  242.8 6.4 %collective-permute-start.42 = (bf16[4,16,512]{2,1,0:T(8,128)(2,1)S(1)}, bf16[4,16,512]{2,1,0:T(8,128)(2,1)S(1)}, u32[]{:S(2)}, u32[]{:S(2)}) collective-permute-start(bf16[4,16,512]{2,1,0:T(8,128)(2,1)S(1)} %get-tuple-element.261), channel_id=1, source_target_pairs={{0,8},{1,9},{2,10},{3,11},{4,12},{5,13},{6,14},{7,15},{8,0},{9,1},... | collective-permute-start | bytes 196616 | tf_op jit(solution)/shard_map/ppermute | solution.py:32
  243.3 8.3 %collective-permute-start.43 = (bf16[4,16,512]{2,1,0:T(8,128)(2,1)S(1)}, bf16[4,16,512]{2,1,0:T(8,128)(2,1)S(1)}, u32[]{:S(2)}, u32[]{:S(2)}) collective-permute-start(bf16[4,16,512]{2,1,0:T(8,128)(2,1)S(1)} %get-tuple-element.260), channel_id=1, source_target_pairs={{0,16},{1,17},{2,18},{3,19},{4,20},{5,21},{6,22},{7,23},{8,24},{9,... | collective-permute-start | bytes 196616 | tf_op jit(solution)/shard_map/ppermute | solution.py:32
  245.1 6.6 %collective-permute-start.44 = (bf16[4,16,512]{2,1,0:T(8,128)(2,1)S(1)}, bf16[4,16,512]{2,1,0:T(8,128)(2,1)S(1)}, u32[]{:S(2)}, u32[]{:S(2)}) collective-permute-start(bf16[4,16,512]{2,1,0:T(8,128)(2,1)S(1)} %get-tuple-element.262), channel_id=1, source_target_pairs={{0,24},{1,25},{2,26},{3,27},{4,28},{5,29},{6,30},{7,31},{8,16},{9,... | collective-permute-start | bytes 196616 | tf_op jit(solution)/shard_map/ppermute | solution.py:32
  (52 other events, 479.8 us)
